TPU v7x, 32 devices: a whole 2x2x4 slice. The times are simulated.
32 devices in a mesh: look: 16 (over z, y, core), swath: 2 (over x).
Axes of the slice: x: 2, y: 2, z: 4, core: 2. Of those that a mesh axis runs over, the one named last changes fastest.
Arguments:
- images: bfloat16 [32, 8, 2, 512, 512], P('look', 'swath'), may hold values from -6 to 6
- patch_weight: float32 [8], P('swath'), may hold values from 1 to 10
- pair_mask: int32 [32, 4], P('look'), may hold values 0 or 1
Outputs:
- drift: float32 [32, 4, 256, 256], P('look', None, 'swath')
All inputs are finite; a program needn't handle non-finite values. No bound on the sum of `pair_mask` on one device may be relied on, other than what follows from the above.
Results may differ from a plain program's by a relative error of at most 0.015.
Values may be sent and summed in bfloat16 or wider, within the bound.
A program may use at most 128 MiB of HBM per device.

v0:
```python
import functools
import math

import jax
import jax.numpy as jnp
import numpy as np
from jax import lax
from jax.experimental import pallas as pl
from jax.experimental.pallas import tpu as pltpu
from jax.sharding import PartitionSpec as P

PIX = 512
BAND = 256
WIN = 256
HALF = PIX // 2


def phases(rows, cols, row_shift, col_shift):
    phase = (rows[:, None] - row_shift) * (cols[None, :] - col_shift) % PIX
    angle = 2.0 * math.pi / PIX * phase
    return np.cos(angle), np.sin(angle)


def forward_tables():
    left, right = [], []
    for parity in (0, 1):
        re, im = phases(np.arange(parity, BAND, 2), np.arange(HALF), BAND // 2, 0)
        im = -im
        left.append(np.block([[re, -im], [im, re]]))
        right.append(np.block([[re.T, im.T], [-im.T, re.T]]))
    return jnp.asarray(np.stack(left), jnp.bfloat16), jnp.asarray(np.stack(right), jnp.bfloat16)


def inverse_tables():
    order = np.concatenate([np.arange(0, BAND, 2), np.arange(1, BAND, 2)])
    re, im = phases(np.arange(WIN), order, WIN // 2, BAND // 2)
    first = np.concatenate([re, im], axis=0)
    second = np.stack([re.T, im.T])
    return jnp.asarray(first, jnp.bfloat16), jnp.asarray(second, jnp.bfloat16)


def dot(left, right):
    return jnp.dot(left, right, preferred_element_type=jnp.float32)


ROWS = 32
MESH = pl.DeviceIdType.MESH


def spectrum_of(img, left_ref, right_ref):
    re0, re1 = img[0, :HALF, :], img[0, HALF:, :]
    im0, im1 = img[1, :HALF, :], img[1, HALF:, :]
    even = dot(left_ref[0], jnp.concatenate([re0 + re1, im0 + im1], axis=0))
    odd = dot(left_ref[1], jnp.concatenate([re0 - re1, im0 - im1], axis=0))
    quarter = BAND // 2
    parts = []
    for at in (0, quarter):
        parts.append(jnp.concatenate([even[at : at + quarter], odd[at : at + quarter]], axis=0))
    plus = [(part[:, :HALF] + part[:, HALF:]).astype(jnp.bfloat16) for part in parts]
    minus = [(part[:, :HALF] - part[:, HALF:]).astype(jnp.bfloat16) for part in parts]
    spec_even = dot(jnp.concatenate(plus, axis=1), right_ref[0]).astype(jnp.bfloat16)
    spec_odd = dot(jnp.concatenate(minus, axis=1), right_ref[1]).astype(jnp.bfloat16)
    return spec_even, spec_odd


def squares_of(spec_even, spec_odd):
    total = spec_even.astype(jnp.float32) ** 2 + spec_odd.astype(jnp.float32) ** 2
    folded = jnp.sum(total.reshape(BAND // 8, 8, BAND), axis=0)
    return folded[:, : BAND // 2] + folded[:, BAND // 2 :]


def cross_into(w_ref, a_ref, b_ref, cre, cim):
    patches = a_ref.shape[0]

    def step(i, carry):
        rows = pl.ds(pl.multiple_of(i * ROWS, ROWS), ROWS)
        re = jnp.zeros((ROWS, BAND), jnp.float32)
        im = jnp.zeros((ROWS, BAND), jnp.float32)
        for p in range(patches):
            weight = w_ref[p]
            ar = a_ref[p, 0, rows, :].astype(jnp.float32) * weight
            ai = a_ref[p, 1, rows, :].astype(jnp.float32) * weight
            br = b_ref[p, 0, rows, :].astype(jnp.float32)
            bi = b_ref[p, 1, rows, :].astype(jnp.float32)
            re += ar * br + ai * bi
            im += ai * br - ar * bi
        cre[rows, :] = re.astype(jnp.bfloat16)
        cim[rows, :] = im.astype(jnp.bfloat16)
        return carry

    lax.fori_loop(0, BAND // ROWS, step, 0)


def halves(first_ref, second_ref, cre, cim):
    from_re = dot(first_ref[...], cre[...]).astype(jnp.bfloat16)
    from_im = dot(first_ref[...], cim[...]).astype(jnp.bfloat16)
    keep = dot(from_re[:WIN], second_ref[0]) - dot(from_re[WIN:], second_ref[1])
    turn = dot(from_im[:WIN], second_ref[1]) + dot(from_im[WIN:], second_ref[0])
    return keep, turn


PAIRS = 7
LAST = PAIRS - 1


def kernel(nlook, nswath, w_ref, mask_ref, img_ref, left_hbm, right_hbm, first_hbm, second_hbm, out_ref, factor_ref,
           left_ref, right_ref, first_ref, second_ref, img, hop, own, near, far, opp, energy, heard, cre, cim, surf, outbox, inbox, turned, backbox,
           table_sem, hop_send, hop_recv, onward_send, forward_send, img_sem, near_send, near_recv, far_send, far_recv, opp_send, opp_recv,
           heard_send, heard_recv, box_send, box_recv, back_send, back_recv):
    looks, patches = img_ref.shape[:2]
    half = nlook // 2
    me, lane = lax.axis_index("look"), lax.axis_index("swath")
    odd = lax.rem(me, 2) == 1
    crossing = lax.rem(me, 4) < 2
    low = me < half
    sent_look = jnp.where(low, 1, 0)
    kept_look = 1 - sent_look

    def device(look_by, swath_by=0):
        return (lax.rem(me + look_by + nlook, nlook), lax.rem(lane + swath_by, nswath))

    def look_at(u):
        return jnp.where(u // patches == 0, sent_look, kept_look)

    def load(u):
        return pltpu.make_async_copy(img_ref.at[look_at(u), u % patches], img.at[u], img_sem.at[u])

    tables = [
        pltpu.make_async_copy(src, dst, table_sem.at[i])
        for i, (src, dst) in enumerate(
            ((left_hbm, left_ref), (right_hbm, right_ref), (first_hbm, first_ref), (second_hbm, second_ref))
        )
    ]
    load(0).start()
    tables[0].start()
    tables[1].start()
    for u in range(1, looks * patches):
        load(u).start()
    tables[2].start()
    tables[3].start()

    barrier = pltpu.get_barrier_semaphore()
    greeted = 0
    for look_by in (0, 1, -1, 2, -2, half):
        for by in range(nswath):
            if look_by or by:
                greeted += 1
                pl.semaphore_signal(barrier, inc=1, device_id=device(look_by, by), device_id_type=MESH)
    for look_by in (3, -3, 4, -4, half - 1, 1 - half, half - 2, 2 - half):
        greeted += 1
        pl.semaphore_signal(barrier, inc=1, device_id=device(look_by), device_id_type=MESH)
    pl.semaphore_wait(barrier, greeted)

    def remote(src, dst, send, recv, to):
        return pltpu.make_async_remote_copy(
            src_ref=src, dst_ref=dst, send_sem=send, recv_sem=recv, device_id=to, device_id_type=MESH
        )

    def to_near(look, p):
        at = look * patches + p
        return remote(own.at[look, p], near.at[look, p], near_send.at[at], near_recv.at[at], device(-1))

    def to_opp(p):
        return remote(own.at[sent_look, p], opp.at[p], opp_send.at[p], opp_recv.at[p], device(half))

    def to_far(p):
        return remote(own.at[0, p], far.at[p], far_send.at[p], far_recv.at[p], device(-2))

    def relay(p):
        sem = far_send.at[patches + p]
        return remote(near.at[0, p], far.at[p], sem, far_recv.at[p], device(-1))

    def to_hop(look, p):
        slot = look * (patches // 2) + p // 2
        return remote(own.at[look, p], hop.at[slot], hop_send.at[slot], hop_recv.at[slot], device(2))

    def onward_near(look, p):
        slot = look * (patches // 2) + p // 2
        at = look * patches + p
        return remote(hop.at[slot], near.at[look, p], onward_send.at[slot], near_recv.at[at], device(-3))

    def onward_far(p):
        slot = p // 2
        return remote(hop.at[slot], far.at[p], onward_send.at[slot], far_recv.at[p], device(-4))

    def forwarded_near(source, look):
        low_one = jnp.logical_and(source == 0, look == 1)
        return jnp.logical_or(low_one, jnp.logical_and(source == half, look == 0))

    def each_forward(p, act):
        at = forward_send.at[p]

        @pl.when(me == 0)
        def _():
            act(remote(opp.at[p], near.at[0, p], at, near_recv.at[p], device(half - 1)))

        @pl.when(me == 1)
        def _():
            act(remote(opp.at[p], far.at[p], at, far_recv.at[p], device(half - 2)))

        @pl.when(me == half)
        def _():
            act(remote(opp.at[p], near.at[1, p], at, near_recv.at[patches + p], device(half - 1)))

    def each_onward(act):
        for look in range(looks):
            for p in range(1, patches, 2):

                @pl.when(jnp.logical_not(jnp.logical_or(odd, forwarded_near(me - 2, look))))
                def _():
                    act(look, p, onward_near(look, p))

                if look == 0:

                    @pl.when(jnp.logical_and(odd, me != half + 3))
                    def _():
                        act(look, p, onward_far(p))

    def each_route(look, p, act):
        via = jnp.logical_and(crossing, p % 2 == 1)
        has_near = jnp.logical_not(forwarded_near(me, look))
        via_near = jnp.logical_and(jnp.logical_and(via, has_near), jnp.logical_not(odd))
        has_far = jnp.logical_and(jnp.logical_and(odd, look == 0), me != half + 1)
        via_far = jnp.logical_and(via, has_far)

        @pl.when(jnp.logical_or(via_near, via_far))
        def _():
            act(to_hop(look, p))

        @pl.when(jnp.logical_and(has_near, jnp.logical_not(via_near)))
        def _():
            act(to_near(look, p))

        @pl.when(jnp.logical_and(has_far, jnp.logical_not(via)))
        def _():
            act(to_far(p))

    def send(u):
        p = u % patches

        @pl.when(u < patches)
        def _():
            to_opp(p).start()

        @pl.when(u >= patches)
        def _():
            early = p < patches // 2
            look = jnp.where(early, sent_look, kept_look)
            for step in range(2):
                patch = 2 * lax.rem(p, patches // 2) + step
                each_route(look, patch, lambda copy: copy.start())

    for look in range(looks):
        energy[look] = jnp.zeros((8, 128), jnp.float32)

    def forward(u, carry):
        @pl.when(u > 0)
        def _():
            send(u - 1)

        look, p = look_at(u), u % patches
        load(u).wait()
        spec_even, spec_odd = spectrum_of(img.at[u], left_ref, right_ref)
        quarter = BAND // 2
        own[look, p, 0, :, :quarter] = spec_even[:, :quarter]
        own[look, p, 0, :, quarter:] = spec_odd[:, :quarter]
        own[look, p, 1, :, :quarter] = spec_even[:, quarter:]
        own[look, p, 1, :, quarter:] = spec_odd[:, quarter:]
        energy[look] += w_ref[p] * squares_of(spec_even, spec_odd)

        return carry

    tables[0].wait()
    tables[1].wait()
    lax.fori_loop(0, looks * patches, forward, 0)
    send(looks * patches - 1)

    tell = []
    for d, look_by in enumerate((0, 1, 2, half)):
        for by in range(nswath):
            if look_by or by:
                tell.append(remote(energy, heard.at[d, by], heard_send.at[d, by], heard_recv.at[d, by],
                                   device(-look_by, by)))
    for copy in tell:
        copy.start()

    rows = WIN // nswath
    mine = pl.ds(pl.multiple_of(lane * rows, rows), rows)

    def outgoing(slot, by):
        at = pl.ds(pl.multiple_of(lax.rem(lane + by, nswath) * rows, rows), rows)
        return remote(outbox.at[slot, at], inbox.at[by - 1, slot], box_send.at[by - 1, slot],
                      box_recv.at[by - 1, slot], device(0, by))

    def returned():
        return remote(turned, backbox, back_send.at[0], back_recv.at[0], device(half))

    def pair(slot, a, b_ref):
        cross_into(w_ref, own.at[a], b_ref, cre, cim)
        keep, turn = halves(first_ref, second_ref, cre, cim)
        value = keep - turn
        surf[slot] = value
        outbox[slot] = value.astype(jnp.bfloat16)
        both = slot is LAST
        if both:
            value = keep + turn
            surf[PAIRS] = value
            outbox[PAIRS] = value.astype(jnp.bfloat16)
        for by in range(1, nswath):
            if both:
                outgoing(PAIRS, by).start()
            outgoing(slot, by).start()

    tables[2].wait()
    tables[3].wait()
    pair(0, 0, own.at[1])

    @pl.when(jnp.logical_not(crossing))
    def _():
        def onward(look, p, copy):
            to_hop(look, p).wait_recv()
            copy.start()

        each_onward(onward)

    late = jnp.logical_and(odd, jnp.logical_not(crossing))

    def ring_pairs():
        ahead = lax.rem(me + 1, nlook)
        first_look = jnp.where(jnp.logical_and(ahead < half, ahead != 0), 1, 0)
        for look in (first_look, 1 - first_look):
            for p in range(patches):
                to_near(look, p).wait_recv()

                @pl.when(jnp.logical_and(odd, look == 0))
                def _():
                    relay(p).start()

            pair(1 + look, 0, near.at[look])
            pair(3 + look, 1, near.at[look])
    @pl.when(jnp.logical_not(late))
    def _():
        ring_pairs()

    for p in range(patches):
        to_opp(p).wait_recv()
        each_forward(p, lambda copy: copy.start())
    pair(LAST, kept_look, opp)

    for copy in tell:
        copy.wait_recv()
    total = []
    for d in range(4):
        for look in range(looks):
            parts = energy[look] if d == 0 else heard[d, 0, look]
            for by in range(1, nswath):
                parts = parts + heard[d, by, look]
            total.append(jnp.sum(parts, axis=(0, 1), keepdims=True))
    scale = BAND * math.sqrt(patches * nswath)

    def factor(look, lag):
        mate = total[look + lag + 1] if lag < 3 else total[3 * looks + look]
        return mask_ref[look, lag].astype(jnp.float32) * scale / jnp.sqrt(total[look] * mate)

    def summed(slot):
        value = surf[slot, mine, :]
        for by in range(1, nswath):
            outgoing(slot, by).wait_recv()
            value = value + inbox[by - 1, slot].astype(jnp.float32)
        return value

    def finish(slot):
        out_ref[slot // 3, slot % 3] = summed(slot)

    turned[...] = summed(PAIRS).astype(jnp.bfloat16)
    for look in range(looks):
        for lag in range(4):
            factor_ref[look, lag : lag + 1, :] = jnp.broadcast_to(factor(look, lag), (1, WIN))
    finish(0)
    returned().start()

    @pl.when(late)
    def _():
        ring_pairs()

    for p in range(patches):
        to_far(p).wait_recv()
    pair(5, 1, far)
    finish(1)
    finish(3)
    kept = summed(PAIRS - 1)
    returned().wait_recv()
    back = backbox[...].astype(jnp.float32)
    out_ref[0, 3] = jnp.where(low, kept, back)
    out_ref[1, 3] = jnp.where(low, back, kept)
    finish(2)
    finish(4)
    finish(5)

    for look in range(looks):
        for p in range(patches):
            each_route(look, p, lambda copy: copy.wait_send())
    for p in range(patches):
        to_opp(p).wait_send()

        @pl.when(odd)
        def _():
            relay(p).wait_send()

        each_forward(p, lambda copy: copy.wait_send())

    @pl.when(jnp.logical_not(crossing))
    def _():
        each_onward(lambda look, p, copy: copy.wait_send())

    for copy in tell:
        copy.wait_send()
    returned().wait_send()
    for slot in range(PAIRS + 1):
        for by in range(1, nswath):
            outgoing(slot, by).wait_send()


def per_device(images, patch_weight, pair_mask):
    nlook = lax.axis_size("look")
    nswath = lax.axis_size("swath")
    looks, patches = images.shape[:2]
    left, right = forward_tables()
    first, second = inverse_tables()
    rows = WIN // nswath
    vmem = pl.BlockSpec(memory_space=pltpu.VMEM)
    smem = pl.BlockSpec(memory_space=pltpu.SMEM)
    dma = pltpu.SemaphoreType.DMA
    unit = (2, BAND, BAND)
    others = max(nswath - 1, 1)
    surfaces, factors = pl.pallas_call(
        functools.partial(kernel, nlook, nswath),
        in_specs=[smem, smem] + [pl.BlockSpec(memory_space=pltpu.HBM)] * 5,
        out_specs=[vmem, vmem],
        out_shape=[
            jax.ShapeDtypeStruct((looks, 4, rows, WIN), jnp.float32),
            jax.ShapeDtypeStruct((looks, 4, WIN), jnp.float32),
        ],
        scratch_shapes=[
            pltpu.VMEM(left.shape, jnp.bfloat16),
            pltpu.VMEM(right.shape, jnp.bfloat16),
            pltpu.VMEM(first.shape, jnp.bfloat16),
            pltpu.VMEM(second.shape, jnp.bfloat16),
            pltpu.VMEM((looks * patches, 2, PIX, PIX), jnp.bfloat16),
            pltpu.VMEM((looks * (patches // 2),) + unit, jnp.bfloat16),
            pltpu.VMEM((looks, patches) + unit, jnp.bfloat16),
            pltpu.VMEM((looks, patches) + unit, jnp.bfloat16),
            pltpu.VMEM((patches,) + unit, jnp.bfloat16),
            pltpu.VMEM((patches,) + unit, jnp.bfloat16),
            pltpu.VMEM((looks, 8, 128), jnp.float32),
            pltpu.VMEM((4, nswath, looks, 8, 128), jnp.float32),
            pltpu.VMEM((BAND, BAND), jnp.bfloat16),
            pltpu.VMEM((BAND, BAND), jnp.bfloat16),
            pltpu.VMEM((PAIRS + 1, WIN, WIN), jnp.float32),
            pltpu.VMEM((PAIRS + 1, WIN, WIN), jnp.bfloat16),
            pltpu.VMEM((others, PAIRS + 1, rows, WIN), jnp.bfloat16),
            pltpu.VMEM((rows, WIN), jnp.bfloat16),
            pltpu.VMEM((rows, WIN), jnp.bfloat16),
            dma((4,)),
            dma((looks * (patches // 2),)),
            dma((looks * (patches // 2),)),
            dma((looks * (patches // 2),)),
            dma((patches,)),
            dma((looks * patches,)),
            dma((looks * patches,)),
            dma((looks * patches,)),
            dma((2 * patches,)),
            dma((patches,)),
            dma((patches,)),
            dma((patches,)),
            dma((4, nswath)),
            dma((4, nswath)),
            dma((others, PAIRS + 1)),
            dma((others, PAIRS + 1)),
            dma((1,)),
            dma((1,)),
        ],
        compiler_params=pltpu.CompilerParams(
            collective_id=0, has_side_effects=True, vmem_limit_bytes=67043328
        ),
        name="autofocus",
    )(patch_weight, pair_mask, images, left, right, first, second)
    return surfaces * factors[:, :, None, :]


def solution(mesh):
    return jax.shard_map(
        per_device,
        mesh=mesh,
        in_specs=(P("look", "swath", None, None, None), P("swath"), P("look", None)),
        out_specs=P("look", None, "swath", None),
        check_vma=False,
    )
```

profile of v0, /device:TPU:13, one launch (start us, length us, event | category | flops | bytes accessed | tf_op | source)
XLA Modules:
  0.0 80.5 jit_solution(9270501230113096736)
XLA Ops:
  0.0 78.2 %autofocus.1 = (f32[2,4,128,256]{3,2,1,0:T(8,128)}, f32[2,4,256]{2,1,0:T(4,128)}) custom-call(f32[4]{0:T(128)} %w_ref.1, s32[2,4]{1,0:T(2,128)} %mask_ref.1, bf16[2,4,2,512,512]{4,3,2,1,0:T(8,128)(2,1)} %img_ref.1, bf16[2,256,512]{2,1,0:T(8,128)(2,1)} %constant.8.clone.left_hbm, bf16[2,512,256]{2,1,0:T(8,128)(2,1)} %constant.9.clone.right_hbm, ...), custom_call_target="tpu_custom_call" | custom-call | tf_op jit(solution)/shard_map/autofocus/pallas_call | solution.py:436
  78.2 2.3 %broadcast_multiply_fusion = f32[2,4,128,256]{3,2,1,0:T(8,128)} fusion(f32[2,4,128,256]{3,2,1,0:T(8,128)} %get-tuple-element.7, f32[2,4,256]{2,1,0:T(4,128)} %get-tuple-element.8), kind=kLoop, calls=%fused_computation | loop fusion | flops 262144 | bytes 2105344 | tf_op jit(solution)/shard_map/mul | solution.py:488
where the time goes:
time: 80.6 us; the launch traced here: 80.5 us
  Pallas kernels  78.2 us (97%)
  other arithmetic  2.28 us (3%)
    pallas_call x1, Pallas kernels, per_device(): pl.pallas_call(functools.partial(kernel, nlook, nswath), in_specs=[smem,...  78.2 us
    mul x1, other arithmetic, per_device(): return surfaces * factors[:, :, None, :]  2.28 us

commit v1 on v0

v1 whole, which is shorter than its diff:
```python
import functools
import math

import jax
import jax.numpy as jnp
import numpy as np
from jax import lax
from jax.experimental import pallas as pl
from jax.experimental.pallas import tpu as pltpu
from jax.sharding import PartitionSpec as P

PIX = 512
BAND = 256
WIN = 256
HALF = PIX // 2


def phases(rows, cols, row_shift, col_shift):
    phase = (rows[:, None] - row_shift) * (cols[None, :] - col_shift) % PIX
    angle = 2.0 * math.pi / PIX * phase
    return np.cos(angle), np.sin(angle)


def forward_tables():
    left, right = [], []
    for parity in (0, 1):
        re, im = phases(np.arange(parity, BAND, 2), np.arange(HALF), BAND // 2, 0)
        im = -im
        left.append(np.block([[re, -im], [im, re]]))
        right.append(np.block([[re.T, im.T], [-im.T, re.T]]))
    return jnp.asarray(np.stack(left), jnp.bfloat16), jnp.asarray(np.stack(right), jnp.bfloat16)


def inverse_tables():
    order = np.concatenate([np.arange(0, BAND, 2), np.arange(1, BAND, 2)])
    re, im = phases(np.arange(WIN), order, WIN // 2, BAND // 2)
    first = np.concatenate([re, im], axis=0)
    second = np.stack([re.T, im.T])
    return jnp.asarray(first, jnp.bfloat16), jnp.asarray(second, jnp.bfloat16)


def dot(left, right):
    return jnp.dot(left, right, preferred_element_type=jnp.float32)


ROWS = 32
MESH = pl.DeviceIdType.MESH


def spectrum_of(img, left_ref, right_ref):
    re0, re1 = img[0, :HALF, :], img[0, HALF:, :]
    im0, im1 = img[1, :HALF, :], img[1, HALF:, :]
    even = dot(left_ref[0], jnp.concatenate([re0 + re1, im0 + im1], axis=0))
    odd = dot(left_ref[1], jnp.concatenate([re0 - re1, im0 - im1], axis=0))
    quarter = BAND // 2
    parts = []
    for at in (0, quarter):
        parts.append(jnp.concatenate([even[at : at + quarter], odd[at : at + quarter]], axis=0))
    plus = [(part[:, :HALF] + part[:, HALF:]).astype(jnp.bfloat16) for part in parts]
    minus = [(part[:, :HALF] - part[:, HALF:]).astype(jnp.bfloat16) for part in parts]
    spec_even = dot(jnp.concatenate(plus, axis=1), right_ref[0]).astype(jnp.bfloat16)
    spec_odd = dot(jnp.concatenate(minus, axis=1), right_ref[1]).astype(jnp.bfloat16)
    return spec_even, spec_odd


def squares_of(spec_even, spec_odd):
    total = spec_even.astype(jnp.float32) ** 2 + spec_odd.astype(jnp.float32) ** 2
    folded = jnp.sum(total.reshape(BAND // 8, 8, BAND), axis=0)
    return folded[:, : BAND // 2] + folded[:, BAND // 2 :]


def cross_into(w_ref, a_ref, b_ref, cre, cim):
    patches = a_ref.shape[0]

    def step(i, carry):
        rows = pl.ds(pl.multiple_of(i * ROWS, ROWS), ROWS)
        re = jnp.zeros((ROWS, BAND), jnp.float32)
        im = jnp.zeros((ROWS, BAND), jnp.float32)
        for p in range(patches):
            weight = w_ref[p]
            ar = a_ref[p, 0, rows, :].astype(jnp.float32) * weight
            ai = a_ref[p, 1, rows, :].astype(jnp.float32) * weight
            br = b_ref[p, 0, rows, :].astype(jnp.float32)
            bi = b_ref[p, 1, rows, :].astype(jnp.float32)
            re += ar * br + ai * bi
            im += ai * br - ar * bi
        cre[rows, :] = re.astype(jnp.bfloat16)
        cim[rows, :] = im.astype(jnp.bfloat16)
        return carry

    lax.fori_loop(0, BAND // ROWS, step, 0)


def halves(first_ref, second_ref, cre, cim):
    from_re = dot(first_ref[...], cre[...]).astype(jnp.bfloat16)
    from_im = dot(first_ref[...], cim[...]).astype(jnp.bfloat16)
    keep = dot(from_re[:WIN], second_ref[0]) - dot(from_re[WIN:], second_ref[1])
    turn = dot(from_im[:WIN], second_ref[1]) + dot(from_im[WIN:], second_ref[0])
    return keep, turn


OWN, NEAR, FAR, OPP, LAST, HIGH, LOW = 0, 2, 4, 5, 7, 10, 13
BUFFERS = 16
OUTS = 8
HERE, ACROSS, LAST_EVEN, LAST_ODD, ZERO, ONE, HALF_EVEN, HALF_ODD = range(8)
TO_MATE, TO_LAST = 1, 2


def pair_step(a, b, out, to=HERE, wait_a=False, wait_b=False, back=None, relay=(0, 0), compute=True, late=False):
    back_to, back_out = back if back else (HERE, 0)
    fields = (
        (a, 16), (b, 16), (int(wait_a), 2), (int(wait_b), 2), (int(compute), 2), (int(back is not None), 2),
        (to, 8), (out, 8), (back_to, 8), (back_out, 8), (relay[0], 4), (relay[1], 16), (int(late), 2),
    )
    code = 0
    for value, base in reversed(fields):
        code = code * base + value
    return code


BASES = (16, 16, 2, 2, 2, 2, 8, 8, 8, 8, 4, 16, 2)


def decode(code):
    values = []
    for base in BASES:
        values.append(lax.rem(code, base))
        code = lax.div(code, base)
    return values


def relay_step(b, relay):
    return pair_step(0, b, 0, wait_b=True, relay=relay, compute=False)


def relay_unit(b, p, relay):
    return pair_step(p, b, 0, relay=relay, compute=False)


def opposite(k):
    return pair_step(OWN + k, OPP + k, 4 * k + 3, wait_b=True, back=(ACROSS, 4 * k + 3))


def step_lists():
    first = [pair_step(OWN, OWN + 1, 0)]
    near_pairs = [
        pair_step(OWN, NEAR, 1, wait_b=True),
        pair_step(OWN + 1, NEAR, 4),
        pair_step(OWN, NEAR + 1, 2, wait_b=True),
        pair_step(OWN + 1, NEAR + 1, 5),
    ]
    on_chip = first + near_pairs
    even = on_chip + [pair_step(OWN + 1, FAR, 6, wait_b=True)]
    to_far = (TO_MATE, FAR)

    def odd(end, late=False):
        return (
            first
            + [
                pair_step(OWN, NEAR, 1, wait_b=True, relay=to_far),
                pair_step(OWN + 1, NEAR, 4),
                pair_step(OWN + 1, FAR, 6, wait_b=True),
                pair_step(OWN, NEAR + 1, 2, wait_b=True, late=late),
                pair_step(OWN + 1, NEAR + 1, 5),
            ]
            + end
        )

    def pass_on(p, which):
        at = (NEAR, NEAR + 1, FAR)[which]
        return relay_unit(LOW + which, p, (TO_LAST, at))

    hub = (
        first
        + near_pairs[:1]
        + [pass_on(0, 0), pass_on(0, 2)]
        + near_pairs[1:]
        + [pass_on(p, which) for p in (1, 2, 3) for which in (0, 2)]
        + [
            pair_step(LAST, HIGH, 6, LAST_EVEN, wait_a=True, wait_b=True),
            pair_step(LOW, HIGH, 3, ZERO, back=(HALF_EVEN, 3)),
            pass_on(0, 1),
            pair_step(LAST + 2, HIGH, 4, LAST_ODD, wait_a=True),
            pair_step(LOW + 2, HIGH + 2, 3, ONE, wait_b=True, back=(HALF_ODD, 3)),
            pass_on(1, 1),
            pair_step(LAST + 2, HIGH + 2, 6, LAST_ODD),
            pass_on(2, 1),
            pass_on(3, 1),
            pair_step(LOW + 1, HIGH + 1, 7, ZERO, wait_b=True, back=(HALF_EVEN, 7)),
            pair_step(LAST + 2, HIGH + 1, 5, LAST_ODD),
            pair_step(LAST + 1, HIGH, 1, LAST_ODD, wait_a=True),
            pair_step(LAST + 1, HIGH + 1, 2, LAST_ODD),
            pair_step(OWN + 1, FAR, 6, wait_b=True),
        ]
    )
    hub_odd = first + [
        pair_step(OWN, NEAR + 1, 2, wait_b=True, relay=(TO_MATE, LAST)),
        pair_step(OWN + 1, NEAR + 1, 5),
        relay_step(NEAR, to_far),
        relay_step(FAR, (TO_MATE, LAST + 1)),
        opposite(1),
        pair_step(OWN, NEAR, 1),
        pair_step(OWN + 1, NEAR, 4),
        pair_step(OWN + 1, FAR, 6),
    ]
    last_even = on_chip + [
        opposite(1),
        pair_step(OPP + 1, FAR, 6, ACROSS, wait_b=True),
    ]
    last_odd = first + [
        relay_step(NEAR, to_far),
        opposite(0),
        pair_step(OPP, NEAR, 1, ACROSS),
        opposite(1),
        pair_step(OPP + 1, NEAR, 4, ACROSS),
        pair_step(OPP + 1, FAR, 6, ACROSS, wait_b=True),
        pair_step(OPP, NEAR + 1, 2, ACROSS, wait_b=True),
        pair_step(OPP + 1, NEAR + 1, 5, ACROSS),
    ]
    return (
        even,
        odd([], late=True),
        even,
        odd([opposite(1)]),
        hub,
        hub_odd,
        last_even,
        last_odd,
        even,
        odd([opposite(1)]),
        even + [opposite(0), opposite(1)],
        odd([opposite(0)], late=True),
        on_chip + [opposite(0)],
        first,
    )


BACK = ((3, 7), (3, 7), (3, 7), (3,), (3, 7), (3,), (3, 6), (1, 2, 4, 5, 6), (3, 7), (3,), (), (7,), (6, 7), (1, 2, 3, 4, 5, 6, 7))
SENT = ((), (1,), (0, 1), (0,), (0, 1), (0,), (0,), (), (), (), (), (1,), (1,), (0, 1))
LEAD = (0, 0, 0, 0, 0, 0, 1, 1, 0, 0, 0, 0, 0, 0)
LATE = (1, 11)
STEPS = max(len(steps) for steps in step_lists())


def pick(index, values):
    result = jnp.int32(values[0]) if isinstance(values[0], int) else values[0]
    for at, value in enumerate(values[1:], 1):
        result = jnp.where(index == at, value, result)
    return result


def bit(mask, at):
    return lax.rem(lax.div(mask, jnp.int32(2**at)), 2) == 1


def kernel(nlook, nswath, w_ref, mask_ref, img_ref, left_hbm, right_hbm, first_hbm, second_hbm, out_ref, factor_ref,
           left_ref, right_ref, first_ref, second_ref, img, spec, energy, heard, cre, cim, surf, outbox, inbox, turned, backbox,
           table_sem, img_sem, near_send, far_send, opp_send, relay_send, spec_recv,
           heard_send, heard_recv, box_send, box_recv, back_send, back_recv):
    looks, patches = img_ref.shape[:2]
    half = nlook // 2
    hub = half - 4
    me, lane = lax.axis_index("look"), lax.axis_index("swath")
    chip, odd = lax.div(me, 2), lax.rem(me, 2)
    low = me < half
    place = jnp.where(low, jnp.int32(1), jnp.int32(5))
    for at, value in ((0, 0), (half // 2 - 2, 2), (half // 2 - 1, 3), (half // 2, 4), (half - 1, 6)):
        place = jnp.where(chip == at, value, place)
    role = 2 * place + odd
    lists = step_lists()
    count = pick(role, [len(steps) for steps in lists])
    codes = [pick(role, [steps[i] if i < len(steps) else 0 for steps in lists]) for i in range(STEPS)]
    backs = pick(role, [sum(2**at for at in outs) for outs in BACK])
    sents = pick(role, [sum(2**at for at in ks) for ks in SENT])
    lead = pick(role, list(LEAD))
    late = functools.reduce(jnp.logical_or, [role == at for at in LATE])

    def device(look_by, swath_by=0):
        return (lax.rem(me + look_by + nlook, nlook), lax.rem(lane + swath_by, nswath))

    def look_at(u):
        return lax.rem(lead + u // patches, looks)

    def load(u):
        return pltpu.make_async_copy(img_ref.at[look_at(u), u % patches], img.at[u], img_sem.at[u])

    tables = [
        pltpu.make_async_copy(src, dst, table_sem.at[i])
        for i, (src, dst) in enumerate(
            ((left_hbm, left_ref), (right_hbm, right_ref), (first_hbm, first_ref), (second_hbm, second_ref))
        )
    ]
    load(0).start()
    tables[0].start()
    tables[1].start()
    for u in range(1, looks * patches):
        load(u).start()
    tables[2].start()
    tables[3].start()

    barrier = pltpu.get_barrier_semaphore()
    greeted = 0
    for look_by in (0, 1, -1, 2, -2, half):
        for by in range(nswath):
            if look_by or by:
                greeted += 1
                pl.semaphore_signal(barrier, inc=1, device_id=device(look_by, by), device_id_type=MESH)
    met = (0, 1, half - 1, half, half + 1)
    meets = functools.reduce(jnp.logical_or, [me == at for at in met])

    @pl.when(me == hub)
    def _():
        for at in met:
            pl.semaphore_signal(barrier, inc=1, device_id=(jnp.int32(at), lane), device_id_type=MESH)

    @pl.when(meets)
    def _():
        pl.semaphore_signal(barrier, inc=1, device_id=(jnp.int32(hub), lane), device_id_type=MESH)

    expected = jnp.where(me == hub, greeted + len(met), jnp.where(meets, greeted + 1, greeted))

    def remote(src, dst, send, recv, to):
        return pltpu.make_async_remote_copy(
            src_ref=src, dst_ref=dst, send_sem=send, recv_sem=recv, device_id=to, device_id_type=MESH
        )

    def arrival(at, p):
        return remote(spec.at[at, p], spec.at[at, p], relay_send.at[at, p], spec_recv.at[at, p], device(-1))

    def to_near(look, p):
        meeting = jnp.logical_or(me == 0, me == half)
        to = jnp.where(meeting, hub, lax.rem(me - 1 + nlook, nlook))
        at = jnp.where(me == 0, LOW, jnp.where(me == half, HIGH, NEAR)) + look
        return remote(spec.at[OWN + look, p], spec.at[at, p], near_send.at[look, p], spec_recv.at[at, p], (to, lane))

    def to_far(look, p):
        meeting = jnp.logical_or(look == 1, jnp.logical_or(me == 1, me == half + 1))
        to = jnp.where(meeting, hub, lax.rem(me - 2 + nlook, nlook))
        at = jnp.where(me == 1, LOW + 2, jnp.where(me == half + 1, HIGH + 2, FAR))
        at = jnp.where(look == 1, LAST + 2, at)
        return remote(spec.at[OWN + look, p], spec.at[at, p], far_send.at[look, p], spec_recv.at[at, p], (to, lane))

    def to_opp(look, p):
        at = OPP + look
        return remote(spec.at[OWN + look, p], spec.at[at, p], opp_send.at[look, p], spec_recv.at[at, p], device(half))

    def relayed(b, p, mate, at):
        to = jnp.where(mate, lax.rem(me - 1 + nlook, nlook), half - 1)
        return remote(spec.at[b, p], spec.at[at, p], relay_send.at[b, p], spec_recv.at[at, p], (to, lane))

    def each_send(look, p, act, all_opp=False):
        has_far = jnp.logical_and(odd == 1, jnp.logical_or(look == 0, me == half - 1))
        has_opp = jnp.where(look == 0, bit(sents, 0), bit(sents, 1))

        @pl.when(has_opp if all_opp else jnp.logical_and(has_opp, jnp.logical_not(late)))
        def _():
            act(to_opp(look, p))

        act(to_near(look, p))

        @pl.when(has_far)
        def _():
            act(to_far(look, p))

    for look in range(looks):
        energy[look] = jnp.zeros((8, 128), jnp.float32)

    def forward(u, carry):
        @pl.when(u == 1)
        def _():
            pl.semaphore_wait(barrier, expected)

        @pl.when(u > 0)
        def _():
            each_send(look_at(u - 1), (u - 1) % patches, lambda copy: copy.start())

        look, p = look_at(u), u % patches
        load(u).wait()
        spec_even, spec_odd = spectrum_of(img.at[u], left_ref, right_ref)
        quarter = BAND // 2
        spec[OWN + look, p, 0, :, :quarter] = spec_even[:, :quarter]
        spec[OWN + look, p, 0, :, quarter:] = spec_odd[:, :quarter]
        spec[OWN + look, p, 1, :, :quarter] = spec_even[:, quarter:]
        spec[OWN + look, p, 1, :, quarter:] = spec_odd[:, quarter:]
        energy[look] += w_ref[p] * squares_of(spec_even, spec_odd)
        return carry

    tables[0].wait()
    tables[1].wait()
    units = looks * patches
    lax.fori_loop(0, units, forward, 0)
    each_send(look_at(units - 1), (units - 1) % patches, lambda copy: copy.start())

    tell = []
    for d, look_by in enumerate((0, 1, 2, half)):
        for by in range(nswath):
            if look_by or by:
                tell.append(remote(energy, heard.at[d, by], heard_send.at[d, by], heard_recv.at[d, by],
                                   device(-look_by, by)))
    for copy in tell:
        copy.start()

    rows = WIN // nswath
    mine = pl.ds(pl.multiple_of(lane * rows, rows), rows)

    def outgoing(slot, by):
        at = pl.ds(pl.multiple_of(lax.rem(lane + by, nswath) * rows, rows), rows)
        return remote(outbox.at[slot, at], inbox.at[by - 1, slot], box_send.at[by - 1, slot],
                      box_recv.at[by - 1, slot], device(0, by))

    def returned(slot, to, out):
        where = pick(to, [me, lax.rem(me + half, nlook), half - 2, half - 1, 0, 1, half, half + 1])
        return remote(turned.at[slot], backbox.at[out], back_send.at[slot], back_recv.at[out], (where, lane))

    def finish(i, slot, to, out):
        value = surf[slot // STEPS * 2 + i % 2, mine, :]
        for by in range(1, nswath):
            outgoing(slot, by).wait_recv()
            value = value + inbox[by - 1, slot].astype(jnp.float32)

        @pl.when(to == HERE)
        def _():
            out_ref[out] = value

        @pl.when(to != HERE)
        def _():
            turned[slot] = value.astype(jnp.bfloat16)
            returned(slot, to, out).start()

    def code_at(i):
        return pick(i, codes)

    tables[2].wait()
    tables[3].wait()

    def step(i, carry):
        a, b, wait_a, wait_b, compute, back, _, _, _, _, relay, relay_at, now = decode(code_at(i))

        @pl.when(jnp.logical_and(compute == 0, wait_b == 0))
        def _():
            arrival(b, a).wait_recv()
            relayed(b, a, relay == TO_MATE, relay_at).start()

        @pl.when(wait_a == 1)
        def _():
            for p in range(patches):
                arrival(a, p).wait_recv()

        @pl.when(wait_b == 1)
        def _():
            for p in range(patches):
                arrival(b, p).wait_recv()

                @pl.when(relay != 0)
                def _():
                    relayed(b, p, relay == TO_MATE, relay_at).start()

        @pl.when(now == 1)
        def _():
            for p in range(patches):
                to_opp(1, p).start()

        @pl.when(compute == 1)
        def _():
            cross_into(w_ref, spec.at[a], spec.at[b], cre, cim)
            keep, turn = halves(first_ref, second_ref, cre, cim)
            value = keep - turn
            surf[i % 2] = value
            outbox[i] = value.astype(jnp.bfloat16)
            value = keep + turn
            surf[2 + i % 2] = value
            outbox[STEPS + i] = value.astype(jnp.bfloat16)
            for by in range(1, nswath):
                outgoing(i, by).start()

            @pl.when(back == 1)
            def _():
                for by in range(1, nswath):
                    outgoing(STEPS + i, by).start()

        @pl.when(i > 0)
        def _():
            settle(i - 1)

        return carry

    def settle(i):
        _, _, _, _, compute, back, to, out, back_to, back_out, _, _, _ = decode(code_at(i))

        @pl.when(compute == 1)
        def _():
            @pl.when(back == 1)
            def _():
                finish(i, STEPS + i, back_to, back_out)

            finish(i, i, to, out)

    lax.fori_loop(0, count, step, 0)
    settle(count - 1)

    for copy in tell:
        copy.wait_recv()
    total = []
    for d in range(4):
        for look in range(looks):
            parts = energy[look] if d == 0 else heard[d, 0, look]
            for by in range(1, nswath):
                parts = parts + heard[d, by, look]
            total.append(jnp.sum(parts, axis=(0, 1), keepdims=True))
    scale = BAND * math.sqrt(patches * nswath)

    def factor(look, lag):
        mate = total[look + lag + 1] if lag < 3 else total[3 * looks + look]
        return mask_ref[look, lag].astype(jnp.float32) * scale / jnp.sqrt(total[look] * mate)

    for look in range(looks):
        for lag in range(4):
            factor_ref[look, lag : lag + 1, :] = jnp.broadcast_to(factor(look, lag), (1, WIN))

    def fetch(out, carry):
        @pl.when(bit_of(backs, out))
        def _():
            remote(turned.at[0], backbox.at[out], back_send.at[0], back_recv.at[out], device(half)).wait_recv()
            out_ref[out] = backbox[out].astype(jnp.float32)

        return carry

    def bit_of(mask, at):
        return pick(at, [lax.rem(lax.div(mask, jnp.int32(2**k)), 2) for k in range(OUTS)]) == 1

    lax.fori_loop(0, OUTS, fetch, 0)

    def drain_sends(u, carry):
        each_send(u // patches, u % patches, lambda copy: copy.wait_send(), True)
        return carry

    lax.fori_loop(0, units, drain_sends, 0)

    def drain_steps(i, carry):
        a, b, _, wait_b, compute, back, to, out, back_to, back_out, relay, relay_at, _ = decode(code_at(i))

        @pl.when(jnp.logical_and(relay != 0, wait_b == 1))
        def _():
            for p in range(patches):
                relayed(b, p, relay == TO_MATE, relay_at).wait_send()

        @pl.when(jnp.logical_and(compute == 0, wait_b == 0))
        def _():
            relayed(b, a, relay == TO_MATE, relay_at).wait_send()

        @pl.when(compute == 1)
        def _():
            for by in range(1, nswath):
                outgoing(i, by).wait_send()

            @pl.when(to != HERE)
            def _():
                returned(i, to, out).wait_send()

            @pl.when(back == 1)
            def _():
                for by in range(1, nswath):
                    outgoing(STEPS + i, by).wait_send()
                returned(STEPS + i, back_to, back_out).wait_send()

        return carry

    lax.fori_loop(0, count, drain_steps, 0)
    for copy in tell:
        copy.wait_send()


def per_device(images, patch_weight, pair_mask):
    nlook = lax.axis_size("look")
    nswath = lax.axis_size("swath")
    looks, patches = images.shape[:2]
    left, right = forward_tables()
    first, second = inverse_tables()
    rows = WIN // nswath
    vmem = pl.BlockSpec(memory_space=pltpu.VMEM)
    smem = pl.BlockSpec(memory_space=pltpu.SMEM)
    dma = pltpu.SemaphoreType.DMA
    unit = (2, BAND, BAND)
    others = max(nswath - 1, 1)
    surfaces, factors = pl.pallas_call(
        functools.partial(kernel, nlook, nswath),
        in_specs=[smem, smem] + [pl.BlockSpec(memory_space=pltpu.HBM)] * 5,
        out_specs=[vmem, vmem],
        out_shape=[
            jax.ShapeDtypeStruct((OUTS, rows, WIN), jnp.float32),
            jax.ShapeDtypeStruct((looks, 4, WIN), jnp.float32),
        ],
        scratch_shapes=[
            pltpu.VMEM(left.shape, jnp.bfloat16),
            pltpu.VMEM(right.shape, jnp.bfloat16),
            pltpu.VMEM(first.shape, jnp.bfloat16),
            pltpu.VMEM(second.shape, jnp.bfloat16),
            pltpu.VMEM((looks * patches, 2, PIX, PIX), jnp.bfloat16),
            pltpu.VMEM((BUFFERS, patches) + unit, jnp.bfloat16),
            pltpu.VMEM((looks, 8, 128), jnp.float32),
            pltpu.VMEM((4, nswath, looks, 8, 128), jnp.float32),
            pltpu.VMEM((BAND, BAND), jnp.bfloat16),
            pltpu.VMEM((BAND, BAND), jnp.bfloat16),
            pltpu.VMEM((4, WIN, WIN), jnp.float32),
            pltpu.VMEM((2 * STEPS, WIN, WIN), jnp.bfloat16),
            pltpu.VMEM((others, 2 * STEPS, rows, WIN), jnp.bfloat16),
            pltpu.VMEM((2 * STEPS, rows, WIN), jnp.bfloat16),
            pltpu.VMEM((OUTS, rows, WIN), jnp.bfloat16),
            dma((4,)),
            dma((looks * patches,)),
            dma((looks, patches)),
            dma((looks, patches)),
            dma((looks, patches)),
            dma((BUFFERS, patches)),
            dma((BUFFERS, patches)),
            dma((4, nswath)),
            dma((4, nswath)),
            dma((others, 2 * STEPS)),
            dma((others, 2 * STEPS)),
            dma((2 * STEPS,)),
            dma((OUTS,)),
        ],
        compiler_params=pltpu.CompilerParams(
            collective_id=0, has_side_effects=True, vmem_limit_bytes=67043328
        ),
        name="autofocus",
    )(patch_weight, pair_mask, images, left, right, first, second)
    return surfaces.reshape(looks, 4, rows, WIN) * factors[:, :, None, :]


def solution(mesh):
    return jax.shard_map(
        per_device,
        mesh=mesh,
        in_specs=(P("look", "swath", None, None, None), P("swath"), P("look", None)),
        out_specs=P("look", None, "swath", None),
        check_vma=False,
    )
```

time: 80.6 us -> 74.2 us (0.921)
  the two profiles are of different devices: /device:TPU:13 before, /device:TPU:9 now
where the time goes in v1:
time: 74.2 us; the launch traced here: 74 us
  Pallas kernels  71.7 us (97%)
  other arithmetic  2.28 us (3%)
    pallas_call x1, Pallas kernels, per_device(): pl.pallas_call(functools.partial(kernel, nlook, nswath), in_specs=[smem,...  71.7 us
    mul x1, other arithmetic, per_device(): return surfaces.reshape(looks, 4, rows, WIN) * factors[:, :, None, :]  2.28 us

profile of v1, /device:TPU:9, one launch (start us, length us, event | category | flops | bytes accessed | tf_op | source)
XLA Modules:
  0.0 74.0 jit_solution(12638931347202850251)
XLA Ops:
  0.0 71.7 %autofocus.1 = (f32[8,128,256]{2,1,0:T(8,128)}, f32[2,4,256]{2,1,0:T(4,128)}) custom-call(f32[4]{0:T(128)} %w_ref.1, s32[2,4]{1,0:T(2,128)} %mask_ref.1, bf16[2,4,2,512,512]{4,3,2,1,0:T(8,128)(2,1)} %img_ref.1, bf16[2,256,512]{2,1,0:T(8,128)(2,1)} %constant.8.clone.left_hbm, bf16[2,512,256]{2,1,0:T(8,128)(2,1)} %constant.9.clone.right_hbm, ...), custom_call_target="tpu_custom_call" | custom-call | tf_op jit(solution)/shard_map/autofocus/pallas_call | solution.py:585
  71.8 2.3 %broadcast_multiply_fusion = f32[2,4,128,256]{3,2,1,0:T(8,128)} fusion(f32[2,4,128,256]{3,2,1,0:T(8,128)} %bitcast.1, f32[2,4,256]{2,1,0:T(4,128)} %get-tuple-element.8), kind=kLoop, calls=%fused_computation | loop fusion | flops 262144 | bytes 2105344 | tf_op jit(solution)/shard_map/mul | solution.py:628

commit v2 on v1

v2 whole, which is shorter than its diff:
```python
import functools
import math

import jax
import jax.numpy as jnp
import numpy as np
from jax import lax
from jax.experimental import pallas as pl
from jax.experimental.pallas import tpu as pltpu
from jax.sharding import PartitionSpec as P

PIX = 512
BAND = 256
WIN = 256
HALF = PIX // 2


def phases(rows, cols, row_shift, col_shift):
    phase = (rows[:, None] - row_shift) * (cols[None, :] - col_shift) % PIX
    angle = 2.0 * math.pi / PIX * phase
    return np.cos(angle), np.sin(angle)


def forward_tables():
    left, right = [], []
    for parity in (0, 1):
        re, im = phases(np.arange(parity, BAND, 2), np.arange(HALF), BAND // 2, 0)
        im = -im
        left.append(np.block([[re, -im], [im, re]]))
        right.append(np.block([[re.T, im.T], [-im.T, re.T]]))
    return jnp.asarray(np.stack(left), jnp.bfloat16), jnp.asarray(np.stack(right), jnp.bfloat16)


def inverse_tables():
    order = np.concatenate([np.arange(0, BAND, 2), np.arange(1, BAND, 2)])
    re, im = phases(np.arange(WIN), order, WIN // 2, BAND // 2)
    first = np.concatenate([re, im], axis=0)
    second = np.stack([re.T, im.T])
    return jnp.asarray(first, jnp.bfloat16), jnp.asarray(second, jnp.bfloat16)


def dot(left, right):
    return jnp.dot(left, right, preferred_element_type=jnp.float32)


ROWS = 32
MESH = pl.DeviceIdType.MESH


def spectrum_of(img, left_ref, right_ref):
    re0, re1 = img[0, :HALF, :], img[0, HALF:, :]
    im0, im1 = img[1, :HALF, :], img[1, HALF:, :]
    even = dot(left_ref[0], jnp.concatenate([re0 + re1, im0 + im1], axis=0))
    odd = dot(left_ref[1], jnp.concatenate([re0 - re1, im0 - im1], axis=0))
    quarter = BAND // 2
    parts = []
    for at in (0, quarter):
        parts.append(jnp.concatenate([even[at : at + quarter], odd[at : at + quarter]], axis=0))
    plus = [(part[:, :HALF] + part[:, HALF:]).astype(jnp.bfloat16) for part in parts]
    minus = [(part[:, :HALF] - part[:, HALF:]).astype(jnp.bfloat16) for part in parts]
    spec_even = dot(jnp.concatenate(plus, axis=1), right_ref[0]).astype(jnp.bfloat16)
    spec_odd = dot(jnp.concatenate(minus, axis=1), right_ref[1]).astype(jnp.bfloat16)
    return spec_even, spec_odd


def squares_of(spec_even, spec_odd):
    total = spec_even.astype(jnp.float32) ** 2 + spec_odd.astype(jnp.float32) ** 2
    folded = jnp.sum(total.reshape(BAND // 8, 8, BAND), axis=0)
    return folded[:, : BAND // 2] + folded[:, BAND // 2 :]


def cross_into(w_ref, a_ref, b_ref, cre, cim):
    patches = a_ref.shape[0]

    def step(i, carry):
        rows = pl.ds(pl.multiple_of(i * ROWS, ROWS), ROWS)
        re = jnp.zeros((ROWS, BAND), jnp.float32)
        im = jnp.zeros((ROWS, BAND), jnp.float32)
        for p in range(patches):
            weight = w_ref[p]
            ar = a_ref[p, 0, rows, :].astype(jnp.float32) * weight
            ai = a_ref[p, 1, rows, :].astype(jnp.float32) * weight
            br = b_ref[p, 0, rows, :].astype(jnp.float32)
            bi = b_ref[p, 1, rows, :].astype(jnp.float32)
            re += ar * br + ai * bi
            im += ai * br - ar * bi
        cre[rows, :] = re.astype(jnp.bfloat16)
        cim[rows, :] = im.astype(jnp.bfloat16)
        return carry

    lax.fori_loop(0, BAND // ROWS, step, 0)


def halves(first_ref, second_ref, cre, cim):
    from_re = dot(first_ref[...], cre[...]).astype(jnp.bfloat16)
    from_im = dot(first_ref[...], cim[...]).astype(jnp.bfloat16)
    keep = dot(from_re[:WIN], second_ref[0]) - dot(from_re[WIN:], second_ref[1])
    turn = dot(from_im[:WIN], second_ref[1]) + dot(from_im[WIN:], second_ref[0])
    return keep, turn


OWN, NEAR, FAR, LOW, OPP, LAST, HIGH = 0, 2, 4, 5, 8, 10, 13
BUFFERS = 16
WHOLE = OPP
OUTS = 8
HERE, ACROSS, LAST_EVEN, LAST_ODD, ZERO, ONE, HALF_EVEN, HALF_ODD = range(8)
TO_MATE, TO_LAST = 1, 2


def pair_step(a, b, out, to=HERE, wait_a=False, wait_b=False, back=None, relay=(0, 0), compute=True, late=False,
              flush=False, direct=False):
    back_to, back_out = back if back else (HERE, 0)
    do = (a, b, int(wait_a), int(wait_b), int(compute), int(back is not None), relay[0], relay[1], int(late),
          int(flush), int(direct))
    end = (int(compute), int(back is not None and not direct), to, out, back_to, back_out)
    return do, end


DO_BASES = (16, 16, 2, 2, 2, 2, 4, 16, 2, 2, 2, 32)
END_BASES = (2, 2, 8, 8, 8, 8, 32)


def encode(values, bases):
    code = 0
    for value, base in zip(reversed(values), reversed(bases), strict=True):
        code = code * base + value
    return code


def decode(code, bases):
    values = []
    for base in bases:
        values.append(lax.rem(code, base))
        code = lax.div(code, base)
    return values


def coded(steps):
    codes, slot = [], 0
    for do, end in steps:
        codes.append((encode(do + (slot,), DO_BASES), encode(end + (slot,), END_BASES)))
        slot += do[4] + do[5]
    return codes


def relay_step(b, relay):
    return pair_step(0, b, 0, wait_b=True, relay=relay, compute=False)


def relay_unit(b, p, relay):
    return pair_step(p, b, 0, relay=relay, compute=False)


def opposite(k, direct=False, flush=False):
    out = 4 * k + 3
    return pair_step(OWN + k, OPP + k, out, wait_b=True, back=(ACROSS, out), direct=direct, flush=flush)


def step_lists():
    first = [pair_step(OWN, OWN + 1, 0)]
    near_pairs = [
        pair_step(OWN, NEAR, 1, wait_b=True),
        pair_step(OWN + 1, NEAR, 4),
        pair_step(OWN, NEAR + 1, 2, wait_b=True),
        pair_step(OWN + 1, NEAR + 1, 5),
    ]
    on_chip = first + near_pairs
    even = on_chip + [pair_step(OWN + 1, FAR, 6, wait_b=True)]
    to_far = (TO_MATE, FAR)

    def odd(end, late=False):
        return (
            first
            + [
                pair_step(OWN, NEAR, 1, wait_b=True, relay=to_far),
                pair_step(OWN + 1, NEAR, 4),
                pair_step(OWN + 1, FAR, 6, wait_b=True),
                pair_step(OWN, NEAR + 1, 2, wait_b=True, late=late),
                pair_step(OWN + 1, NEAR + 1, 5),
            ]
            + end
        )

    def pass_on(p, which):
        at = (NEAR, NEAR + 1, FAR)[which]
        return relay_unit(LOW + which, p, (TO_LAST, at))

    def pass_both(p):
        return [pass_on(p, 0), pass_on(p, 2)]

    hub = (
        pass_both(0)
        + first
        + near_pairs[:2]
        + pass_both(1)
        + near_pairs[2:]
        + pass_both(2)
        + pass_both(3)
        + [
            pair_step(LOW, HIGH, 3, ZERO, wait_b=True, back=(HALF_EVEN, 3)),
            pass_on(0, 1),
            pair_step(LOW + 2, HIGH + 2, 3, ONE, wait_b=True, back=(HALF_ODD, 3)),
            pass_on(1, 1),
            pass_on(2, 1),
            pair_step(LAST, HIGH, 6, LAST_EVEN, wait_a=True),
            pass_on(3, 1),
            pair_step(LAST + 2, HIGH, 4, LAST_ODD, wait_a=True),
            pair_step(LAST + 2, HIGH + 2, 6, LAST_ODD),
            pair_step(LAST + 1, HIGH, 1, LAST_ODD, wait_a=True),
            pair_step(LAST + 1, HIGH + 1, 2, LAST_ODD, wait_b=True),
            pair_step(LAST + 2, HIGH + 1, 5, LAST_ODD),
            pair_step(LOW + 1, HIGH + 1, 7, ZERO, back=(HALF_EVEN, 7)),
            pair_step(OWN + 1, FAR, 6, wait_b=True, flush=True),
        ]
    )
    hub_odd = first + [
        pair_step(OWN, NEAR + 1, 2, wait_b=True, relay=(TO_MATE, LAST)),
        pair_step(OWN + 1, NEAR + 1, 5),
        pair_step(OWN + 1, FAR, 6, wait_b=True, relay=(TO_MATE, LAST + 1)),
        relay_step(NEAR, to_far),
        opposite(1, True),
        pair_step(OWN, NEAR, 1),
        pair_step(OWN + 1, NEAR, 4),
    ]
    last_even = on_chip + [
        opposite(1),
        pair_step(0, FAR, 0, wait_b=True, compute=False, late=True),
        pair_step(OPP + 1, FAR, 6, ACROSS),
    ]
    last_odd = first + [
        relay_step(NEAR, to_far),
        opposite(0),
        pair_step(OPP, NEAR, 1, ACROSS),
        opposite(1),
        pair_step(OPP + 1, NEAR, 4, ACROSS),
        pair_step(OPP + 1, FAR, 6, ACROSS, wait_b=True),
        pair_step(OPP, NEAR + 1, 2, ACROSS, wait_b=True, flush=True),
        pair_step(OPP + 1, NEAR + 1, 5, ACROSS),
    ]
    return (
        even,
        odd([], late=True),
        even,
        odd([opposite(1, True)]),
        hub,
        hub_odd,
        last_even,
        last_odd,
        even,
        odd([opposite(1, True)]),
        even + [opposite(0), opposite(1, True, True)],
        odd([opposite(0)], late=True),
        on_chip + [opposite(0, True)],
        first,
    )


BACK = ((3, 7), (3,), (3,), (3,), (3,), (3,), (6,), (1, 2, 4, 5, 6), (3, 7), (3,), (), (), (6, 7), (1, 2, 3, 4, 5, 6, 7))
PARTS_OF = {1: 7, 2: 7, 4: 7, 6: 3, 11: 7}
PARTS_BY = (3, 5, 9, 10, 12)
HELD_BACK, FREES = {7: 2, 10: 1}, (6, 11)
SENT = ((), (1,), (0, 1), (0,), (0, 1), (0,), (0,), (), (), (), (), (1,), (1,), (0, 1))
LATE, LATE_NEAR = (1, 11), 6
AHEAD = 2
LAG = 2
HELD = 4
STEPS = max(len(steps) for steps in step_lists())
RESULTS = [sum(end[0] + end[1] for _, end in steps) for steps in step_lists()]
RETURNS = [sum(int(end[2] != HERE) + end[1] for _, end in steps) for steps in step_lists()]
SLOTS = max(sum(do[4] + do[5] for do, _ in steps) for steps in step_lists())


def looks_sent(role, patches):
    relayed = sum((patches if do[3] else 1) for do, _ in step_lists()[role] if do[6])
    return 2 + role % 2 + int(role == 7) + len(SENT[role]) + relayed // patches


def pick(index, values):
    result = jnp.int32(values[0]) if isinstance(values[0], int) else values[0]
    for at, value in enumerate(values[1:], 1):
        result = jnp.where(index == at, value, result)
    return result


def bit(mask, at):
    return lax.rem(lax.div(mask, jnp.int32(2**at)), 2) == 1


def kernel(nlook, nswath, w_ref, mask_ref, img_ref, left_hbm, right_hbm, first_hbm, second_hbm, out_hbm, factor_hbm,
           left_ref, right_ref, first_ref, second_ref, img, spec, energy, heard, cre, cim, surf, outbox, inbox, turned, backbox, parts, final, factors,
           table_sem, img_sem, unit_send, spec_recv,
           heard_send, heard_recv, box_send, box_recv, back_send, back_recv, parts_send, parts_recv, out_sem, ready, go):
    looks, patches = img_ref.shape[:2]
    half = nlook // 2
    hub = half - 4
    me, lane = lax.axis_index("look"), lax.axis_index("swath")
    chip, odd = lax.div(me, 2), lax.rem(me, 2)
    lead = jnp.where(chip == half // 2 - 1, 1, 0)

    def device(look_by, swath_by=0):
        return (lax.rem(me + look_by + nlook, nlook), lax.rem(lane + swath_by, nswath))

    def look_at(u):
        return lax.rem(lead + u // patches, looks)

    def load(u):
        return pltpu.make_async_copy(img_ref.at[look_at(u), u % patches], img.at[u], img_sem.at[u % AHEAD])

    tables = [
        pltpu.make_async_copy(src, dst, table_sem.at[i])
        for i, (src, dst) in enumerate(
            ((left_hbm, left_ref), (right_hbm, right_ref), (first_hbm, first_ref), (second_hbm, second_ref))
        )
    ]
    units = looks * patches
    load(0).start()
    tables[0].start()
    tables[1].start()
    for u in range(1, AHEAD):
        load(u).start()

    barrier = pltpu.get_barrier_semaphore()
    greeted = 0
    behind = []
    for look_by in (0, 1, -1, 2, -2, half):
        for by in range(nswath):
            if look_by or by:
                greeted += 1
                to = device(look_by, by)
                if look_by in (1, 2, half):
                    later = jnp.logical_and(to[0] < 2, me >= half)
                    behind.append((later, to))

                    @pl.when(jnp.logical_not(later))
                    def _():
                        pl.semaphore_signal(barrier, inc=1, device_id=to, device_id_type=MESH)
                else:
                    pl.semaphore_signal(barrier, inc=1, device_id=to, device_id_type=MESH)
    met = (0, 1, half - 1, half, half + 1)
    meets = functools.reduce(jnp.logical_or, [me == at for at in met])

    @pl.when(me == hub)
    def _():
        for at in met:
            pl.semaphore_signal(barrier, inc=1, device_id=(jnp.int32(at), lane), device_id_type=MESH)

    @pl.when(meets)
    def _():
        pl.semaphore_signal(barrier, inc=1, device_id=(jnp.int32(hub), lane), device_id_type=MESH)

    expected = jnp.where(me == hub, greeted + len(met), jnp.where(meets, greeted + 1, greeted))
    missing = jnp.where(me == 0, 3 * nswath, jnp.where(me == 1, 2 * nswath, 0))

    place = jnp.where(me < half, jnp.int32(1), jnp.int32(5))
    for at, value in ((0, 0), (half // 2 - 2, 2), (half // 2 - 1, 3), (half // 2, 4), (half - 1, 6)):
        place = jnp.where(chip == at, value, place)
    role = 2 * place + odd
    sents = pick(role, [sum(2**at for at in ks) for ks in SENT])
    late = functools.reduce(jnp.logical_or, [role == at for at in LATE])
    held_back = functools.reduce(jnp.logical_or, [role == at for at in HELD_BACK])
    left_out = functools.reduce(lambda n, r: jnp.where(role == r, HELD_BACK[r], n), HELD_BACK, 0)

    def remote(src, dst, send, recv, to):
        return pltpu.make_async_remote_copy(
            src_ref=src, dst_ref=dst, send_sem=send, recv_sem=recv, device_id=to, device_id_type=MESH
        )

    def unit(src, at, p, to):
        recv = jnp.where(at < WHOLE, (at - NEAR) * patches + p, (WHOLE - NEAR) * patches + at - WHOLE)
        return remote(spec.at[src, p], spec.at[at, p], unit_send.at[0], spec_recv.at[recv], to)

    def arrival(at, p):
        return unit(at, at, p, device(-1))

    def arrival_of_look(at):
        recv = (WHOLE - NEAR) * patches + at - WHOLE
        return remote(spec.at[at], spec.at[at], unit_send.at[0], spec_recv.at[recv], device(-1))

    def to_near(look, p):
        meeting = jnp.logical_or(me == 0, me == half)
        to = jnp.where(meeting, hub, lax.rem(me - 1 + nlook, nlook))
        at = jnp.where(me == 0, LOW, jnp.where(me == half, HIGH, NEAR)) + look
        return unit(OWN + look, at, p, (to, lane))

    def to_far(look, p):
        meeting = jnp.logical_or(look == 1, jnp.logical_or(me == 1, me == half + 1))
        to = jnp.where(meeting, hub, lax.rem(me - 2 + nlook, nlook))
        at = jnp.where(me == 1, LOW + 2, jnp.where(me == half + 1, HIGH + 2, FAR))
        at = jnp.where(look == 1, LAST + 2, at)
        return unit(OWN + look, at, p, (to, lane))

    def to_opp(look, p):
        return unit(OWN + look, OPP + look, p, device(half))

    def relayed(b, p, mate, at):
        to = jnp.where(mate, lax.rem(me - 1 + nlook, nlook), half - 1)
        return unit(b, at, p, (to, lane))

    def each_send(look, p):
        has_far = jnp.logical_and(odd == 1, jnp.logical_or(look == 0, me == half - 1))
        has_opp = jnp.where(look == 0, bit(sents, 0), bit(sents, 1))

        @pl.when(jnp.logical_and(has_opp, jnp.logical_not(late)))
        def _():
            to_opp(look, p).start()

        held = jnp.logical_and(role == LATE_NEAR, look == 0)

        @pl.when(jnp.logical_not(held))
        def _():
            to_near(look, p).start()

        @pl.when(has_far)
        def _():
            to_far(look, p).start()

    for look in range(looks):
        energy[look] = jnp.zeros((8, 128), jnp.float32)

    def forward(u, carry):
        @pl.when(u == 1)
        def _():
            pl.semaphore_wait(barrier, expected - missing)
            for later, to in behind:

                @pl.when(later)
                def _():
                    pl.semaphore_signal(ready, inc=1, device_id=to, device_id_type=MESH)

        @pl.when(u > 0)
        def _():
            each_send(look_at(u - 1), (u - 1) % patches)

        look, p = look_at(u), u % patches
        load(u).wait()

        @pl.when(u < units - AHEAD)
        def _():
            load(u + AHEAD).start()

        @pl.when(u == units - AHEAD)
        def _():
            tables[2].start()
            tables[3].start()

        spec_even, spec_odd = spectrum_of(img.at[u], left_ref, right_ref)
        quarter = BAND // 2
        spec[OWN + look, p, 0, :, :quarter] = spec_even[:, :quarter]
        spec[OWN + look, p, 0, :, quarter:] = spec_odd[:, :quarter]
        spec[OWN + look, p, 1, :, :quarter] = spec_even[:, quarter:]
        spec[OWN + look, p, 1, :, quarter:] = spec_odd[:, quarter:]
        energy[look] += w_ref[p] * squares_of(spec_even, spec_odd)
        return carry

    tables[0].wait()
    tables[1].wait()
    lax.fori_loop(0, units, forward, 0)
    each_send(look_at(units - 1), (units - 1) % patches)

    tell = []
    for d, look_by in enumerate((0, 1, 2, half)):
        for by in range(nswath):
            if look_by or by:
                tell.append(remote(energy, heard.at[d * nswath + by], heard_send.at[0], heard_recv.at[0],
                                   device(-look_by, by)))

    @pl.when(me < 2)
    def _():
        pl.semaphore_wait(ready, missing)

    for copy in tell:
        copy.start()

    lists = [coded(steps) for steps in step_lists()]
    count = pick(role, [len(steps) for steps in lists])
    backs = pick(role, [sum(2**at for at in outs) for outs in BACK])
    dos, ends = (
        [pick(role, [steps[i][which] if i < len(steps) else 0 for steps in lists]) for i in range(STEPS)]
        for which in (0, 1)
    )

    rows = WIN // nswath
    mine = pl.ds(pl.multiple_of(lane * rows, rows), rows)

    def outgoing(slot, by):
        at = pl.ds(pl.multiple_of(lax.rem(lane + by, nswath) * rows, rows), rows)
        return remote(outbox.at[slot, at], inbox.at[by - 1, slot], box_send.at[by - 1],
                      box_recv.at[by - 1, slot], device(0, by))

    def part(slot, by):
        at = pl.ds(pl.multiple_of(lax.rem(lane + by, nswath) * rows, rows), rows)
        return remote(outbox.at[slot, at], parts.at[by], parts_send.at[0], parts_recv.at[0], device(half, by))

    def returned(slot, to, out):
        where = pick(to, [me, lax.rem(me + half, nlook), half - 2, half - 1, 0, 1, half, half + 1])
        return remote(turned.at[slot], backbox.at[out], back_send.at[0], back_recv.at[out], (where, lane))

    def finish(i, at, slot, to, out):
        value = surf[at, mine, :]
        for by in range(1, nswath):
            outgoing(slot, by).wait_recv()
            value = value + inbox[by - 1, slot].astype(jnp.float32)

        @pl.when(to == HERE)
        def _():
            final[out] = value
            put(out).start()

        @pl.when(to != HERE)
        def _():
            turned[slot] = value.astype(jnp.bfloat16)

            @pl.when(jnp.logical_not(jnp.logical_and(held_back, i < count - left_out)))
            def _():
                returned(slot, to, out).start()

    def send_late(p):
        @pl.when(role == LATE_NEAR)
        def _():
            to_near(0, p).start()

        @pl.when(role != LATE_NEAR)
        def _():
            to_opp(1, p).start()

    def put(out):
        return pltpu.make_async_copy(final.at[out], out_hbm.at[out], out_sem.at[0])

    put_factor = pltpu.make_async_copy(factors, factor_hbm, table_sem.at[0])

    tables[2].wait()
    tables[3].wait()

    def step(i, carry):
        a, b, wait_a, wait_b, compute, back, relay, relay_at, now, flush, direct, slot = decode(pick(i, dos), DO_BASES)

        @pl.when(flush == 1)
        def _():
            for at, code in enumerate(carry):
                settle(i - LAG + at, code)

        carry = tuple(jnp.where(flush == 1, 0, code) for code in carry)

        @pl.when(i == count - 1)
        def _():
            weigh()

        @pl.when(jnp.logical_and(compute == 0, wait_b == 0))
        def _():
            arrival(b, a).wait_recv()
            relayed(b, a, relay == TO_MATE, relay_at).start()

        @pl.when(wait_a == 1)
        def _():
            arrival_of_look(a).wait_recv()

        @pl.when(jnp.logical_and(wait_b == 1, b >= WHOLE))
        def _():
            arrival_of_look(b).wait_recv()

        @pl.when(jnp.logical_and(wait_b == 1, b < WHOLE))
        def _():
            for p in range(patches):
                arrival(b, p).wait_recv()

                @pl.when(relay != 0)
                def _():
                    relayed(b, p, relay == TO_MATE, relay_at).start()

                if p >= patches - 2:

                    @pl.when(jnp.logical_and(now == 1, (role == LATE_NEAR) == (p == patches - 1)))
                    def _():
                        for q in range(patches):
                            send_late(q)

        @pl.when(jnp.logical_and(held_back, i == count - 1))
        def _():
            release()

        @pl.when(compute == 1)
        def _():
            cross_into(w_ref, spec.at[a], spec.at[b], cre, cim)
            keep, turn = halves(first_ref, second_ref, cre, cim)
            value = keep - turn
            surf[i % HELD] = value
            outbox[slot] = value.astype(jnp.bfloat16)
            value = keep + turn
            surf[HELD + i % HELD] = value
            for by in range(1, nswath):
                outgoing(slot, by).start()

            @pl.when(back == 1)
            def _():
                outbox[slot + 1] = value.astype(jnp.bfloat16)

                @pl.when(direct == 1)
                def _():
                    for by in range(nswath):
                        part(slot + 1, by).start()

                @pl.when(direct == 0)
                def _():
                    for by in range(1, nswath):
                        outgoing(slot + 1, by).start()

        settle(i - LAG, carry[0])
        return (*carry[1:], pick(i, ends))

    def release():
        pl.semaphore_wait(go, 1)
        for r, leaves in HELD_BACK.items():

            @pl.when(role == r)
            def _():
                slot = 0
                for do, end in step_lists()[r][:-leaves]:
                    if do[4] and end[2] != HERE:
                        returned(slot, jnp.int32(end[2]), end[3]).start()
                    if end[1]:
                        returned(slot + 1, jnp.int32(end[4]), end[5]).start()
                    slot += do[4] + do[5]

    def settle(i, code):
        compute, back, to, out, back_to, back_out, slot = decode(code, END_BASES)

        @pl.when(compute == 1)
        def _():
            at = lax.rem(i + HELD, HELD)

            @pl.when(back == 1)
            def _():
                finish(i, HELD + at, slot + 1, back_to, back_out)

            finish(i, at, slot, to, out)

    def all_heard():
        told = heard.at[pl.ds(1, 4 * nswath - 1)]
        return remote(told, told, heard_send.at[0], heard_recv.at[0], device(-1))

    def weigh():
        all_heard().wait_recv()
        total = []
        for d in range(4):
            for look in range(looks):
                parts = energy[look] if d == 0 else heard[d * nswath, look]
                for by in range(1, nswath):
                    parts = parts + heard[d * nswath + by, look]
                total.append(jnp.sum(parts, axis=(0, 1), keepdims=True))
        scale = BAND * math.sqrt(patches * nswath)

        def factor(look, lag):
            mate = total[look + lag + 1] if lag < 3 else total[3 * looks + look]
            return mask_ref[look, lag].astype(jnp.float32) * scale / jnp.sqrt(total[look] * mate)

        for look in range(looks):
            for lag in range(4):
                factors[look, lag : lag + 1, :] = jnp.broadcast_to(factor(look, lag), (1, WIN))
        put_factor.start()

    def fetch(out, carry):
        @pl.when(bit_of(backs, out))
        def _():
            remote(turned.at[0], backbox.at[out], back_send.at[0], back_recv.at[out], device(half)).wait_recv()
            final[out] = backbox[out].astype(jnp.float32)
            put(out).start()

        return carry

    def bit_of(mask, at):
        return pick(at, [lax.rem(lax.div(mask, jnp.int32(2**k)), 2) for k in range(OUTS)]) == 1

    def by_role(counts, act):
        mine_of = pick(role, list(counts))
        for n in sorted(set(counts)):
            if n:

                @pl.when(mine_of == n)
                def _():
                    act(n)

    def drain_units(n):
        sent = spec.at[pl.ds(0, n)]
        remote(sent, sent, unit_send.at[0], spec_recv.at[0], device(-1)).wait_send()

    def drain_boxes(n):
        for by in range(1, nswath):
            sent = inbox.at[by - 1, pl.ds(0, n)]
            remote(sent, sent, box_send.at[by - 1], box_recv.at[by - 1, 0], device(0, by)).wait_send()

    def drain_returns(n):
        sent = turned.at[pl.ds(0, n)]
        remote(sent, sent, back_send.at[0], back_recv.at[0], device(half)).wait_send()

    pending = lax.fori_loop(0, count, step, (jnp.int32(0),) * LAG)
    for at, code in enumerate(pending):
        settle(count - LAG + at, code)
    by_role([looks_sent(r, patches) for r in range(len(RESULTS))], drain_units)

    @pl.when(functools.reduce(jnp.logical_or, [role == at for at in FREES]))
    def _():
        to = jnp.where(odd == 1, me - 1, me + 1)
        pl.semaphore_signal(go, inc=1, device_id=(to, lane), device_id_type=MESH)

    lax.fori_loop(0, OUTS, fetch, 0)
    place_of = pick(role, [PARTS_OF.get(r, OUTS) for r in range(len(RESULTS))])
    all_parts = remote(parts, parts, parts_send.at[0], parts_recv.at[0], device(half))

    @pl.when(place_of < OUTS)
    def _():
        all_parts.wait_recv()
        value = parts[0].astype(jnp.float32)
        for by in range(1, nswath):
            value = value + parts[by].astype(jnp.float32)
        final[place_of] = value
        put(place_of).start()

    @pl.when(functools.reduce(jnp.logical_or, [role == r for r in PARTS_BY]))
    def _():
        all_parts.wait_send()

    by_role(RESULTS, drain_boxes)
    by_role(RETURNS, drain_returns)
    all_heard().wait_send()
    put_factor.wait()
    pltpu.make_async_copy(final, out_hbm, out_sem.at[0]).wait()


def per_device(images, patch_weight, pair_mask):
    nlook = lax.axis_size("look")
    nswath = lax.axis_size("swath")
    looks, patches = images.shape[:2]
    left, right = forward_tables()
    first, second = inverse_tables()
    rows = WIN // nswath
    hbm = pl.BlockSpec(memory_space=pltpu.HBM)
    smem = pl.BlockSpec(memory_space=pltpu.SMEM)
    dma = pltpu.SemaphoreType.DMA
    unit = (2, BAND, BAND)
    others = max(nswath - 1, 1)
    operands = (patch_weight, pair_mask, images, left, right, first, second)
    surfaces, scales = pl.pallas_call(
        functools.partial(kernel, nlook, nswath),
        in_specs=[smem, smem] + [hbm] * 5,
        out_specs=[pl.BlockSpec(memory_space=pl.ANY)] * 2,
        out_shape=[
            jax.ShapeDtypeStruct((OUTS, rows, WIN), jnp.float32),
            jax.ShapeDtypeStruct((looks, 4, WIN), jnp.float32),
        ],
        scratch_shapes=[
            pltpu.VMEM(left.shape, jnp.bfloat16),
            pltpu.VMEM(right.shape, jnp.bfloat16),
            pltpu.VMEM(first.shape, jnp.bfloat16),
            pltpu.VMEM(second.shape, jnp.bfloat16),
            pltpu.VMEM((looks * patches, 2, PIX, PIX), jnp.bfloat16),
            pltpu.VMEM((BUFFERS, patches) + unit, jnp.bfloat16),
            pltpu.VMEM((looks, 8, 128), jnp.float32),
            pltpu.VMEM((4 * nswath, looks, 8, 128), jnp.float32),
            pltpu.VMEM((BAND, BAND), jnp.bfloat16),
            pltpu.VMEM((BAND, BAND), jnp.bfloat16),
            pltpu.VMEM((2 * HELD, WIN, WIN), jnp.float32),
            pltpu.VMEM((SLOTS, WIN, WIN), jnp.bfloat16),
            pltpu.VMEM((others, SLOTS, rows, WIN), jnp.bfloat16),
            pltpu.VMEM((SLOTS, rows, WIN), jnp.bfloat16),
            pltpu.VMEM((OUTS, rows, WIN), jnp.bfloat16),
            pltpu.VMEM((nswath, rows, WIN), jnp.bfloat16),
            pltpu.VMEM((OUTS, rows, WIN), jnp.float32),
            pltpu.VMEM((looks, 4, WIN), jnp.float32),
            dma((4,)),
            dma((AHEAD,)),
            dma((1,)),
            dma(((WHOLE - NEAR) * patches + BUFFERS - WHOLE,)),
            dma((1,)),
            dma((1,)),
            dma((others,)),
            dma((others, SLOTS)),
            dma((1,)),
            dma((OUTS,)),
            dma((1,)),
            dma((1,)),
            dma((1,)),
            pltpu.SemaphoreType.REGULAR,
            pltpu.SemaphoreType.REGULAR,
        ],
        compiler_params=pltpu.CompilerParams(
            collective_id=0, has_side_effects=True, vmem_limit_bytes=52224 << 10
        ),
        name="autofocus",
    )(*[pltpu.with_memory_space_constraint(x, pltpu.HBM) for x in operands])
    return surfaces.reshape(looks, 4, rows, WIN) * scales[:, :, None, :]


def solution(mesh):
    return jax.shard_map(
        per_device,
        mesh=mesh,
        in_specs=(P("look", "swath", None, None, None), P("swath"), P("look", None)),
        out_specs=P("look", None, "swath", None),
        check_vma=False,
    )
```

time: 74.2 us -> 62.3 us (0.84)
  Pallas kernels: 71.7 us -> 61 us
  other arithmetic: 2.28 us -> 1.07 us
    pallas_call x1, Pallas kernels: 71.7 us -> 61 us  [per_device(): pl.pallas_call(functools.partial(kernel, nlook, nswath), in_specs=[smem,...]
    mul x1, other arithmetic: 2.28 us -> 1.07 us  [per_device(): return surfaces.reshape(looks, 4, rows, WIN) * scales[:, :, None, :]]
where the time goes in v2:
time: 62.3 us; the launch traced here: 62 us
  Pallas kernels  61 us (98%)
  other arithmetic  1.07 us (2%)
    pallas_call x1, Pallas kernels, per_device(): pl.pallas_call(functools.partial(kernel, nlook, nswath), in_specs=[smem,...  61 us

profile of v2, /device:TPU:9, one launch (start us, length us, event | category | flops | bytes accessed | tf_op | source)
XLA Modules:
  0.0 62.0 jit_solution(13533899923881569439)
XLA Ops:
  0.0 61.0 %autofocus.1 = (f32[8,128,256]{2,1,0:T(8,128)S(1)}, f32[2,4,256]{2,1,0:T(4,128)S(1)}) custom-call(f32[4]{0:T(128)} %w_ref.1, s32[2,4]{1,0:T(2,128)} %mask_ref.1, bf16[2,4,2,512,512]{4,3,2,1,0:T(8,128)(2,1)} %img_ref.1, bf16[2,256,512]{2,1,0:T(8,128)(2,1)} %constant.8.clone.left_hbm, bf16[2,512,256]{2,1,0:T(8,128)(2,1)} %constant.9.clone.right_hbm, ...), custom_call_target="tpu_custom_call" | custom-call | tf_op jit(solution)/shard_map/autofocus/pallas_call | solution.py:742
  61.0 1.1 %broadcast_multiply_fusion = f32[2,4,128,256]{3,2,1,0:T(8,128)} fusion(f32[2,4,128,256]{3,2,1,0:T(8,128)S(1)} %bitcast.1, f32[2,4,256]{2,1,0:T(4,128)S(1)} %get-tuple-element.8), kind=kLoop, calls=%fused_computation | loop fusion | flops 262144 | bytes 2105344 | tf_op jit(solution)/shard_map/mul | solution.py:790

commit v3 on v2

--- a/solution.py
+++ b/solution.py
@@ -91,6 +91,30 @@
     lax.fori_loop(0, BAND // ROWS, step, 0)
 
 
+def add_patch(w_ref, a_ref, b_ref, p, acc, cre=None, cim=None):
+    def step(i, carry):
+        rows = pl.ds(pl.multiple_of(i * ROWS, ROWS), ROWS)
+        weight = w_ref[p]
+        ar = a_ref[p, 0, rows, :].astype(jnp.float32) * weight
+        ai = a_ref[p, 1, rows, :].astype(jnp.float32) * weight
+        br = b_ref[p, 0, rows, :].astype(jnp.float32)
+        bi = b_ref[p, 1, rows, :].astype(jnp.float32)
+        re = ar * br + ai * bi
+        im = ai * br - ar * bi
+        if p:
+            re = acc[0, rows, :] + re
+            im = acc[1, rows, :] + im
+        if cre is None:
+            acc[0, rows, :] = re
+            acc[1, rows, :] = im
+        else:
+            cre[rows, :] = re.astype(jnp.bfloat16)
+            cim[rows, :] = im.astype(jnp.bfloat16)
+        return carry
+
+    lax.fori_loop(0, BAND // ROWS, step, 0)
+
+
 def halves(first_ref, second_ref, cre, cim):
     from_re = dot(first_ref[...], cre[...]).astype(jnp.bfloat16)
     from_im = dot(first_ref[...], cim[...]).astype(jnp.bfloat16)
@@ -99,24 +123,24 @@
     return keep, turn
 
 
-OWN, NEAR, FAR, LOW, OPP, LAST, HIGH = 0, 2, 4, 5, 8, 10, 13
-BUFFERS = 16
-WHOLE = OPP
+OWN, NEAR, FAR, LOW, OPP, LAST, HIGH = 0, 2, 4, 5, 5, 8, 11
+BUFFERS = 14
+WHOLE = LAST
 OUTS = 8
 HERE, ACROSS, LAST_EVEN, LAST_ODD, ZERO, ONE, HALF_EVEN, HALF_ODD = range(8)
 TO_MATE, TO_LAST = 1, 2
 
 
 def pair_step(a, b, out, to=HERE, wait_a=False, wait_b=False, back=None, relay=(0, 0), compute=True, late=False,
-              flush=False, direct=False):
+              flush=False, direct=False, adds=0, ends=0):
     back_to, back_out = back if back else (HERE, 0)
     do = (a, b, int(wait_a), int(wait_b), int(compute), int(back is not None), relay[0], relay[1], int(late),
-          int(flush), int(direct))
+          int(flush), int(direct), adds, ends)
     end = (int(compute), int(back is not None and not direct), to, out, back_to, back_out)
     return do, end
 
 
-DO_BASES = (16, 16, 2, 2, 2, 2, 4, 16, 2, 2, 2, 32)
+DO_BASES = (16, 16, 2, 2, 2, 2, 4, 16, 2, 2, 2, 4, 4, 32)
 END_BASES = (2, 2, 8, 8, 8, 8, 32)
 
 
@@ -153,7 +177,8 @@
 
 def opposite(k, direct=False, flush=False):
     out = 4 * k + 3
-    return pair_step(OWN + k, OPP + k, out, wait_b=True, back=(ACROSS, out), direct=direct, flush=flush)
+    return pair_step(OWN + k, OPP + k, out, wait_b=True, back=(ACROSS, out), direct=direct, flush=flush,
+                     adds=int(direct), ends=int(direct))
 
 
 def step_lists():
@@ -206,21 +231,20 @@
             pass_on(3, 1),
             pair_step(LAST + 2, HIGH, 4, LAST_ODD, wait_a=True),
             pair_step(LAST + 2, HIGH + 2, 6, LAST_ODD),
+            pair_step(LOW + 1, HIGH + 1, 7, ZERO, wait_b=True, back=(HALF_EVEN, 7)),
+            pair_step(LAST + 2, HIGH + 1, 5, LAST_ODD),
             pair_step(LAST + 1, HIGH, 1, LAST_ODD, wait_a=True),
-            pair_step(LAST + 1, HIGH + 1, 2, LAST_ODD, wait_b=True),
-            pair_step(LAST + 2, HIGH + 1, 5, LAST_ODD),
-            pair_step(LOW + 1, HIGH + 1, 7, ZERO, back=(HALF_EVEN, 7)),
-            pair_step(OWN + 1, FAR, 6, wait_b=True, flush=True),
+            pair_step(LAST + 1, HIGH + 1, 2, LAST_ODD),
+            pair_step(OWN + 1, FAR, 6, wait_b=True, flush=True, adds=1, ends=1),
         ]
     )
     hub_odd = first + [
         pair_step(OWN, NEAR + 1, 2, wait_b=True, relay=(TO_MATE, LAST)),
         pair_step(OWN + 1, NEAR + 1, 5),
         pair_step(OWN + 1, FAR, 6, wait_b=True, relay=(TO_MATE, LAST + 1)),
-        relay_step(NEAR, to_far),
-        opposite(1, True),
-        pair_step(OWN, NEAR, 1),
-        pair_step(OWN + 1, NEAR, 4),
+        pair_step(OWN, NEAR, 1, wait_b=True, relay=to_far, adds=2, ends=1),
+        pair_step(OWN + 1, OPP + 1, 7, wait_b=True, back=(ACROSS, 7), direct=True),
+        pair_step(OWN + 1, NEAR, 4, ends=2),
     ]
     last_even = on_chip + [
         opposite(1),
@@ -287,7 +311,7 @@
 
 
 def kernel(nlook, nswath, w_ref, mask_ref, img_ref, left_hbm, right_hbm, first_hbm, second_hbm, out_hbm, factor_hbm,
-           left_ref, right_ref, first_ref, second_ref, img, spec, energy, heard, cre, cim, surf, outbox, inbox, turned, backbox, parts, final, factors,
+           left_ref, right_ref, first_ref, second_ref, img, spec, energy, heard, cre, cim, acc, surf, outbox, inbox, turned, backbox, parts, final, factors,
            table_sem, img_sem, unit_send, spec_recv,
            heard_send, heard_recv, box_send, box_recv, back_send, back_recv, parts_send, parts_recv, out_sem, ready, go):
     looks, patches = img_ref.shape[:2]
@@ -307,35 +331,39 @@
         return pltpu.make_async_copy(img_ref.at[look_at(u), u % patches], img.at[u], img_sem.at[u % AHEAD])
 
     tables = [
-        pltpu.make_async_copy(src, dst, table_sem.at[i])
+        pltpu.make_async_copy(src, dst, table_sem.at[i % 2])
         for i, (src, dst) in enumerate(
             ((left_hbm, left_ref), (right_hbm, right_ref), (first_hbm, first_ref), (second_hbm, second_ref))
         )
     ]
+    barrier = pltpu.get_barrier_semaphore()
+    behind = []
+
+    def greet(look_bys):
+        count = 0
+        for look_by in look_bys:
+            for by in range(nswath):
+                if look_by or by:
+                    count += 1
+                    to = device(look_by, by)
+                    if look_by in (1, 2, half):
+                        ends_of_low = jnp.logical_or(to[0] < 2, jnp.logical_and(to[0] >= half - 2, to[0] < half))
+                        later = jnp.logical_and(ends_of_low, me >= half)
+                        behind.append((later, to))
+
+                        @pl.when(jnp.logical_not(later))
+                        def _():
+                            pl.semaphore_signal(barrier, inc=1, device_id=to, device_id_type=MESH)
+                    else:
+                        pl.semaphore_signal(barrier, inc=1, device_id=to, device_id_type=MESH)
+        return count
+
+    greeted = greet((half,))
     units = looks * patches
     load(0).start()
     tables[0].start()
     tables[1].start()
-    for u in range(1, AHEAD):
-        load(u).start()
-
-    barrier = pltpu.get_barrier_semaphore()
-    greeted = 0
-    behind = []
-    for look_by in (0, 1, -1, 2, -2, half):
-        for by in range(nswath):
-            if look_by or by:
-                greeted += 1
-                to = device(look_by, by)
-                if look_by in (1, 2, half):
-                    later = jnp.logical_and(to[0] < 2, me >= half)
-                    behind.append((later, to))
-
-                    @pl.when(jnp.logical_not(later))
-                    def _():
-                        pl.semaphore_signal(barrier, inc=1, device_id=to, device_id_type=MESH)
-                else:
-                    pl.semaphore_signal(barrier, inc=1, device_id=to, device_id_type=MESH)
+    greeted += greet((0, 1, -1, 2, -2))
     met = (0, 1, half - 1, half, half + 1)
     meets = functools.reduce(jnp.logical_or, [me == at for at in met])
 
@@ -349,14 +377,15 @@
         pl.semaphore_signal(barrier, inc=1, device_id=(jnp.int32(hub), lane), device_id_type=MESH)
 
     expected = jnp.where(me == hub, greeted + len(met), jnp.where(meets, greeted + 1, greeted))
-    missing = jnp.where(me == 0, 3 * nswath, jnp.where(me == 1, 2 * nswath, 0))
+    on_last = chip == half // 2 - 1
+    missing = jnp.where(me == 0, 3 * nswath, jnp.where(me == 1, 2 * nswath, jnp.where(on_last, nswath, 0)))
 
     place = jnp.where(me < half, jnp.int32(1), jnp.int32(5))
     for at, value in ((0, 0), (half // 2 - 2, 2), (half // 2 - 1, 3), (half // 2, 4), (half - 1, 6)):
         place = jnp.where(chip == at, value, place)
     role = 2 * place + odd
     sents = pick(role, [sum(2**at for at in ks) for ks in SENT])
-    late = functools.reduce(jnp.logical_or, [role == at for at in LATE])
+    late = jnp.logical_or(role == LATE[0], jnp.logical_and(role == LATE[1], chip >= half // 2 + 2))
     held_back = functools.reduce(jnp.logical_or, [role == at for at in HELD_BACK])
     left_out = functools.reduce(lambda n, r: jnp.where(role == r, HELD_BACK[r], n), HELD_BACK, 0)
 
@@ -427,12 +456,21 @@
                 def _():
                     pl.semaphore_signal(ready, inc=1, device_id=to, device_id_type=MESH)
 
+        @pl.when(jnp.logical_and(on_last, u == patches + 1))
+        def _():
+            pl.semaphore_wait(ready, missing)
+
         @pl.when(u > 0)
         def _():
             each_send(look_at(u - 1), (u - 1) % patches)
 
         look, p = look_at(u), u % patches
         load(u).wait()
+
+        @pl.when(u == 0)
+        def _():
+            for first in range(1, AHEAD):
+                load(first).start()
 
         @pl.when(u < units - AHEAD)
         def _():
@@ -519,7 +557,7 @@
         def _():
             to_near(0, p).start()
 
-        @pl.when(role != LATE_NEAR)
+        @pl.when(late)
         def _():
             to_opp(1, p).start()
 
@@ -532,7 +570,7 @@
     tables[3].wait()
 
     def step(i, carry):
-        a, b, wait_a, wait_b, compute, back, relay, relay_at, now, flush, direct, slot = decode(pick(i, dos), DO_BASES)
+        a, b, wait_a, wait_b, compute, back, relay, relay_at, now, flush, direct, adds, ends_at, slot = decode(pick(i, dos), DO_BASES)
 
         @pl.when(flush == 1)
         def _():
@@ -540,10 +578,6 @@
                 settle(i - LAG + at, code)
 
         carry = tuple(jnp.where(flush == 1, 0, code) for code in carry)
-
-        @pl.when(i == count - 1)
-        def _():
-            weigh()
 
         @pl.when(jnp.logical_and(compute == 0, wait_b == 0))
         def _():
@@ -566,6 +600,16 @@
                 @pl.when(relay != 0)
                 def _():
                     relayed(b, p, relay == TO_MATE, relay_at).start()
+
+                if p < patches - 1:
+
+                    @pl.when(adds >= 1)
+                    def _():
+                        add_patch(w_ref, spec.at[a], spec.at[b], p, acc.at[0])
+
+                    @pl.when(adds == 2)
+                    def _():
+                        add_patch(w_ref, spec.at[OWN + 1], spec.at[b], p, acc.at[1])
 
                 if p >= patches - 2:
 
@@ -580,7 +624,14 @@
 
         @pl.when(compute == 1)
         def _():
-            cross_into(w_ref, spec.at[a], spec.at[b], cre, cim)
+            @pl.when(ends_at >= 1)
+            def _():
+                add_patch(w_ref, spec.at[a], spec.at[b], patches - 1, acc.at[ends_at - 1], cre, cim)
+
+            @pl.when(ends_at == 0)
+            def _():
+                cross_into(w_ref, spec.at[a], spec.at[b], cre, cim)
+
             keep, turn = halves(first_ref, second_ref, cre, cim)
             value = keep - turn
             surf[i % HELD] = value
@@ -596,13 +647,17 @@
 
                 @pl.when(direct == 1)
                 def _():
-                    for by in range(nswath):
+                    for by in reversed(range(nswath)):
                         part(slot + 1, by).start()
 
                 @pl.when(direct == 0)
                 def _():
                     for by in range(1, nswath):
                         outgoing(slot + 1, by).start()
+
+        @pl.when(i == count - 1)
+        def _():
+            weigh()
 
         settle(i - LAG, carry[0])
         return (*carry[1:], pick(i, ends))
@@ -658,17 +713,12 @@
                 factors[look, lag : lag + 1, :] = jnp.broadcast_to(factor(look, lag), (1, WIN))
         put_factor.start()
 
-    def fetch(out, carry):
-        @pl.when(bit_of(backs, out))
+    def fetch(out):
+        @pl.when(bit(backs, out))
         def _():
             remote(turned.at[0], backbox.at[out], back_send.at[0], back_recv.at[out], device(half)).wait_recv()
             final[out] = backbox[out].astype(jnp.float32)
             put(out).start()
-
-        return carry
-
-    def bit_of(mask, at):
-        return pick(at, [lax.rem(lax.div(mask, jnp.int32(2**k)), 2) for k in range(OUTS)]) == 1
 
     def by_role(counts, act):
         mine_of = pick(role, list(counts))
@@ -702,7 +752,8 @@
         to = jnp.where(odd == 1, me - 1, me + 1)
         pl.semaphore_signal(go, inc=1, device_id=(to, lane), device_id_type=MESH)
 
-    lax.fori_loop(0, OUTS, fetch, 0)
+    for out in range(OUTS):
+        fetch(out)
     place_of = pick(role, [PARTS_OF.get(r, OUTS) for r in range(len(RESULTS))])
     all_parts = remote(parts, parts, parts_send.at[0], parts_recv.at[0], device(half))
 
@@ -758,6 +809,7 @@
             pltpu.VMEM((4 * nswath, looks, 8, 128), jnp.float32),
             pltpu.VMEM((BAND, BAND), jnp.bfloat16),
             pltpu.VMEM((BAND, BAND), jnp.bfloat16),
+            pltpu.VMEM((2, 2, BAND, BAND), jnp.float32),
             pltpu.VMEM((2 * HELD, WIN, WIN), jnp.float32),
             pltpu.VMEM((SLOTS, WIN, WIN), jnp.bfloat16),
             pltpu.VMEM((others, SLOTS, rows, WIN), jnp.bfloat16),
@@ -766,7 +818,7 @@
             pltpu.VMEM((nswath, rows, WIN), jnp.bfloat16),
             pltpu.VMEM((OUTS, rows, WIN), jnp.float32),
             pltpu.VMEM((looks, 4, WIN), jnp.float32),
-            dma((4,)),
+            dma((2,)),
             dma((AHEAD,)),
             dma((1,)),
             dma(((WHOLE - NEAR) * patches + BUFFERS - WHOLE,)),

time: 62.3 us -> 60.8 us (0.976)
  Pallas kernels: 61 us -> 59.5 us
    pallas_call x1, Pallas kernels: 61 us -> 59.5 us  [per_device(): pl.pallas_call(functools.partial(kernel, nlook, nswath), in_specs=[smem,...]
where the time goes in v3:
time: 60.8 us; the launch traced here: 60.6 us
  Pallas kernels  59.5 us (98%)
  other arithmetic  1.07 us (2%)
    pallas_call x1, Pallas kernels, per_device(): pl.pallas_call(functools.partial(kernel, nlook, nswath), in_specs=[smem,...  59.5 us

profile of v3, /device:TPU:9, one launch (start us, length us, event | category | flops | bytes accessed | tf_op | source)
XLA Modules:
  0.0 60.6 jit_solution(12594956775423322149)
XLA Ops:
  0.0 59.5 %autofocus.1 = (f32[8,128,256]{2,1,0:T(8,128)S(1)}, f32[2,4,256]{2,1,0:T(4,128)S(1)}) custom-call(f32[4]{0:T(128)} %w_ref.1, s32[2,4]{1,0:T(2,128)} %mask_ref.1, bf16[2,4,2,512,512]{4,3,2,1,0:T(8,128)(2,1)} %img_ref.1, bf16[2,256,512]{2,1,0:T(8,128)(2,1)} %constant.8.clone.left_hbm, bf16[2,512,256]{2,1,0:T(8,128)(2,1)} %constant.9.clone.right_hbm, ...), custom_call_target="tpu_custom_call" | custom-call | tf_op jit(solution)/shard_map/autofocus/pallas_call | solution.py:793
  59.6 1.1 %broadcast_multiply_fusion = f32[2,4,128,256]{3,2,1,0:T(8,128)} fusion(f32[2,4,128,256]{3,2,1,0:T(8,128)S(1)} %bitcast.1, f32[2,4,256]{2,1,0:T(4,128)S(1)} %get-tuple-element.8), kind=kLoop, calls=%fused_computation | loop fusion | flops 262144 | bytes 2105344 | tf_op jit(solution)/shard_map/mul | solution.py:842
